TPU v7x, 1024 devices: a whole 4x4x32 slice. The times are simulated.
1024 devices in a mesh: rep: 64 (over z_lo, x, core), dom: 16 (over z_hi, y).
Axes of the slice: x: 4, y: 4, z: 32 (z_hi: 4, z_lo: 8; z = z_hi * 8 + z_lo), core: 2. Of those that a mesh axis runs over, the one named last changes fastest.
Arguments:
- block_input: bfloat16 [1024, 8, 16, 320], P(('rep', 'dom')), may hold values from -36 to 36
- cotangent: bfloat16 [1024, 8, 16, 320], P(('rep', 'dom')), may hold values from -6 to 6
- timesteps: int32 [1024], P(('rep', 'dom')), may hold values from 0 to 999
- owner_map: int32 [16], replicated, may hold values from 0 to 15, each once
- time_weight: bfloat16 [1280, 320], replicated, may hold values from -0.15625 to 0.15625
- first_weight: bfloat16 [2880, 320], P('dom'), may hold values from -0.109375 to 0.109375
- second_weight: bfloat16 [2880, 320], P('dom'), may hold values from -0.109375 to 0.109375
Outputs:
- block_output: bfloat16 [1024, 8, 16, 320], P(('rep', 'dom'))
- first_grad: float32 [2880, 320], P('dom')
- second_grad: float32 [2880, 320], P('dom')
Inputs may be any that keep to these rules, and one draw needn't show every extreme that they name: `owner_map`: each dom index holds exactly one block.
All inputs are finite; a program needn't handle non-finite values.
Results may differ from a plain program's by a relative error of at most 0.0064.
Values may be sent and summed in bfloat16 or wider, within the bound.
A program may use at most 32 MiB of HBM per device.

v0:
```python
import math

import jax
import jax.numpy as jnp
from jax import lax
from jax.sharding import PartitionSpec as P

C = 320
GROUPS = 32
TEMB = 1280
HEIGHT = 8
WIDTH = 16


norm_eps = 1e-05


def columns(activation):
    padded = jnp.pad(activation, ((1, 1), (1, 1), (0, 0)))
    pieces = []
    for row_tap in range(3):
        for col_tap in range(3):
            pieces.append(padded[row_tap : row_tap + HEIGHT, col_tap : col_tap + WIDTH, :])
    return jnp.concatenate(pieces, axis=-1).reshape(HEIGHT * WIDTH, 9 * C)


def tap_window(activation, first_tap, tap_count):
    padded = jnp.pad(activation, ((1, 1), (1, 1), (0, 0)))
    pieces = []
    for offset in range(tap_count):
        tap_index = first_tap + offset
        pieces.append(
            lax.dynamic_slice(padded, (tap_index // 3, tap_index % 3, 0), (HEIGHT, WIDTH, C))
        )
    return jnp.concatenate(pieces, axis=-1).reshape(HEIGHT * WIDTH, tap_count * C)


def spread_back(gathered):
    framed = jnp.pad(gathered.reshape(HEIGHT, WIDTH, 9, C), ((1, 1), (1, 1), (0, 0), (0, 0)))
    result = jnp.zeros((HEIGHT, WIDTH, C), jnp.float32)
    for row_tap in range(3):
        for col_tap in range(3):
            result = (
                result
                + framed[
                    2 - row_tap : 2 - row_tap + HEIGHT,
                    2 - col_tap : 2 - col_tap + WIDTH,
                    3 * row_tap + col_tap,
                    :,
                ]
            )
    return result.reshape(HEIGHT * WIDTH, C)


def group_norm(values):
    grouped = values.reshape(HEIGHT * WIDTH, GROUPS, C // GROUPS)
    center = jnp.mean(grouped, axis=(0, 2), keepdims=True)
    spread = jnp.mean(jnp.square(grouped - center), axis=(0, 2), keepdims=True)
    inverse_std = lax.rsqrt(spread + norm_eps)
    return (((grouped - center) * inverse_std).reshape(HEIGHT * WIDTH, C), inverse_std)


def norm_back(incoming, normed, inverse_std):
    grouped_grad = incoming.reshape(HEIGHT * WIDTH, GROUPS, C // GROUPS)
    grouped_norm = normed.reshape(HEIGHT * WIDTH, GROUPS, C // GROUPS)
    mean_grad = jnp.mean(grouped_grad, axis=(0, 2), keepdims=True)
    mean_prod = jnp.mean(grouped_grad * grouped_norm, axis=(0, 2), keepdims=True)
    return (inverse_std * (grouped_grad - mean_grad - grouped_norm * mean_prod)).reshape(
        HEIGHT * WIDTH, C
    )


def time_bias(timestep, time_weight):
    half_dim = TEMB // 2
    frequency = jnp.exp(-math.log(10000.0) * jnp.arange(half_dim, dtype=jnp.float32) / half_dim)
    angles = timestep.astype(jnp.float32) * frequency
    embedded = jnp.concatenate([jnp.cos(angles), jnp.sin(angles)])
    activated = jax.nn.silu(embedded).astype(jnp.bfloat16)
    return jnp.dot(activated[None, :], time_weight, preferred_element_type=jnp.float32)


def logical_order(stored, owner_map, group_size, block_rows):
    blocks = stored.reshape(group_size, block_rows, C)
    return jnp.take(blocks, owner_map, axis=0).reshape(9 * C, C)


def transposed_product(cols_rows, grad_rows):
    return lax.dot_general(
        cols_rows, grad_rows, (((0,), (0,)), ((), ())), preferred_element_type=jnp.float32
    )


def second_owner_sum(term_rounded, inverse, group_size, block_rows):
    stored_blocks = jnp.take(term_rounded.reshape(group_size, block_rows, C), inverse, axis=0)
    arrived = lax.all_to_all(stored_blocks, "dom", split_axis=0, concat_axis=0, tiled=True)
    return jnp.sum(arrived.astype(jnp.float32), axis=0)


def body(block_input, cotangent, timesteps, owner_map, time_weight, first_weight, second_weight):
    pixels = HEIGHT * WIDTH
    group_size = lax.axis_size("dom")
    block_rows = first_weight.shape[0]
    samples_total = lax.axis_size("rep") * group_size
    block_ids = jnp.arange(group_size, dtype=jnp.int32)
    matches = (owner_map[None, :] == block_ids[:, None]).astype(jnp.int32)
    inverse = jnp.sum(matches * block_ids[None, :], axis=1)
    source = block_input[0].astype(jnp.float32).reshape(pixels, C)
    normed, unused_std = group_norm(source)
    first_act = jax.nn.silu(normed).astype(jnp.bfloat16)
    first_cols = columns(first_act.reshape(HEIGHT, WIDTH, C))
    bias_row = time_bias(timesteps[0], time_weight)
    first_stored, second_stored = (
        lax.all_gather(first_weight, "dom", axis=0, tiled=True),
        lax.all_gather(second_weight, "dom", axis=0, tiled=True),
    )
    first_logic = logical_order(first_stored, owner_map, group_size, block_rows)
    first_conv = jnp.dot(first_cols, first_logic, preferred_element_type=jnp.float32) + bias_row
    second_logic = logical_order(second_stored, owner_map, group_size, block_rows)
    second_norm, second_std = group_norm(first_conv)
    second_act = jax.nn.silu(second_norm).astype(jnp.bfloat16)
    second_cols = columns(second_act.reshape(HEIGHT, WIDTH, C))
    block_output = (
        source + jnp.dot(second_cols, second_logic, preferred_element_type=jnp.float32)
    ).astype(jnp.bfloat16)
    upstream = cotangent[0].reshape(pixels, C)
    second_term = transposed_product(second_cols, upstream).astype(jnp.bfloat16)
    second_owned = second_owner_sum(second_term, inverse, group_size, block_rows)
    second_back = lax.dot_general(
        upstream, second_logic, (((1,), (1,)), ((), ())), preferred_element_type=jnp.float32
    )
    act_grad = spread_back(second_back)
    gate_value = jax.nn.sigmoid(second_norm)
    norm_grad = act_grad * gate_value * (1.0 + second_norm * (1.0 - gate_value))
    conv_grad = norm_back(norm_grad, second_norm, second_std).astype(jnp.bfloat16)
    own_logical = inverse[lax.axis_index("dom")]
    tap_count = min(9, block_rows // C + 2)
    first_tap = jnp.minimum(own_logical * block_rows // C, 9 - tap_count)
    column_start = own_logical * block_rows - first_tap * C
    act_piece = lax.all_gather(first_act.reshape(1, HEIGHT, WIDTH, C), "dom", axis=0, tiled=True)
    grad_piece = lax.all_gather(conv_grad.reshape(1, HEIGHT, WIDTH, C), "dom", axis=0, tiled=True)

    def add_one(total, pair):
        act_one, grad_one = pair
        window = tap_window(act_one, first_tap, tap_count)
        owned_cols = lax.dynamic_slice_in_dim(window, column_start, block_rows, 1)
        term = transposed_product(owned_cols, grad_one.reshape(pixels, C))
        return (
            total + lax.optimization_barrier(term.astype(jnp.bfloat16)).astype(jnp.float32),
            None,
        )

    total, unused_rest = lax.scan(
        add_one, jnp.zeros((block_rows, C), jnp.float32), (act_piece, grad_piece)
    )
    second_total, first_total = lax.psum((second_owned, total), "rep")
    return (
        block_output.reshape(1, HEIGHT, WIDTH, C),
        first_total / samples_total,
        second_total / samples_total,
    )


def solution(mesh):
    placed = (
        P(("rep", "dom"), None, None, None),
        P(("rep", "dom"), None, None, None),
        P(("rep", "dom")),
        P(),
        P(),
        P("dom", None),
        P("dom", None),
    )
    return jax.shard_map(
        body,
        mesh=mesh,
        in_specs=placed,
        out_specs=(P(("rep", "dom"), None, None, None), P("dom", None), P("dom", None)),
        check_vma=False,
    )
```

profile of v0, /device:TPU:1, one launch (start us, length us, event | category | flops | bytes accessed | tf_op | source)
XLA Modules:
  0.0 1675.7 jit_solution(7213730692887893920)
XLA Ops:
  19.0 179.2 %all-gather.13.cloned.1.call-done = bf16[16,180,320]{2,1,0:T(8,128)(2,1)} async-done(((bf16[1,180,320]{2,1,0:T(8,128)(2,1)}), bf16[16,180,320]{2,1,0:T(8,128)(2,1)}) %all-gather.13.cloned.1.call-update) | async-done | bytes 1843216 | tf_op jit(solution)/shard_map/all_gather | solution.py:114
  198.3 3.9 gather_fusion.1
  202.2 168.8 %all-gather.11.cloned.1.call-done = bf16[16,180,320]{2,1,0:T(8,128)(2,1)} async-done(((bf16[1,180,320]{2,1,0:T(8,128)(2,1)}), bf16[16,180,320]{2,1,0:T(8,128)(2,1)}) %all-gather.11.cloned.1.call-update) | async-done | bytes 1843216 | tf_op jit(solution)/shard_map/all_gather | solution.py:113
  371.0 3.9 gather_fusion
  374.9 5.0 broadcast_select_fusion.1
  379.9 2.8 reshape.192
  382.6 2.2 fusion.16
  385.9 2.8 reshape.195
  388.7 2.8 convolution_bitcast_fusion
  391.4 3.0 copy.89
  394.4 3.1 reshape.197
  397.5 7.2 fusion.9
  416.4 2.3 pad_slice_fusion.8
  439.0 2.9 convolution_convert_fusion.1
  441.9 9.5 reshape.249
  451.4 4.6 copy.93
  456.0 3.9 gather_fusion.2
  459.9 3.4 broadcast_select_fusion
  463.3 14.0 all-to-all-start
  477.4 91.6 %all-gather.7.cloned.1.call-done = bf16[16,8,16,320]{3,2,1,0:T(8,128)(2,1)} async-done(((bf16[1,8,16,320]{3,2,1,0:T(8,128)(2,1)}), bf16[16,8,16,320]{3,2,1,0:T(8,128)(2,1)}) %all-gather.7.cloned.1.call-update) | async-done | bytes 1310736 | tf_op jit(solution)/shard_map/all_gather | solution.py:139
  569.0 251.7 %all-gather.9.cloned.1.call-done = bf16[16,8,16,320]{3,2,1,0:T(8,128)(2,1)} async-done(((bf16[1,8,16,320]{3,2,1,0:T(8,128)(2,1)}), bf16[16,8,16,320]{3,2,1,0:T(8,128)(2,1)}) %all-gather.9.cloned.1.call-update) | async-done | bytes 1310736 | tf_op jit(solution)/shard_map/all_gather | solution.py:140
  820.7 39.5 %while.14 = (s32[]{:T(128)}, f32[180,320]{1,0:T(8,128)S(1)}, bf16[16,8,16,320]{3,2,1,0:T(8,128)(2,1)}, s32[]{:T(128)}, s32[]{:T(128)}, /*index=5*/s32[]{:T(128)}...) while((s32[]{:T(128)}, f32[180,320]{1,0:T(8,128)S(1)}, ...), condition=%wide.region_14.16_spmd.clone, body=%wide.region_13.15_spmd.clone.sunk | while | flops 15303683 | bytes 1756315 | solution.py:152
  860.2 2.9 convert_reduce_fusion
  866.0 799.8 %all-reduce.7.cloned.1.call-done = (f32[180,320]{1,0:T(8,128)}, f32[180,320]{1,0:T(8,128)}) async-done(((f32[180,320]{1,0:T(8,128)}, f32[180,320]{1,0:T(8,128)}), (f32[180,320]{1,0:T(8,128)}, f32[180,320]{1,0:T(8,128)})) %all-reduce.7.cloned.1.call-update) | async-done | bytes 460816 | tf_op jit(solution)/shard_map/psum | solution.py:155
  (217 shorter events, 88.0 us)
Async XLA Ops:
  7.2 11.1 copy-start
  7.2 191.1 %all-gather.13.cloned.1.call-start = ((), (), s32[]{:S(2)}) async-start(), calls=%async_computation.4 | async-start | bytes 2402304 | tf_op jit(solution)/shard_map/all_gather | solution.py:114
  7.9 363.1 %all-gather.11.cloned.1.call-start = ((), (), s32[]{:S(2)}) async-start(), calls=%async_computation.3 | async-start | bytes 2402304 | tf_op jit(solution)/shard_map/all_gather | solution.py:113
  8.7 560.3 %all-gather.7.cloned.1.call-start = ((), (), s32[]{:S(2)}) async-start(), calls=%async_computation.1 | async-start | bytes 1671168 | tf_op jit(solution)/shard_map/all_gather | solution.py:139
  13.1 807.6 %all-gather.9.cloned.1.call-start = ((), (), s32[]{:S(2)}) async-start(), calls=%async_computation.2 | async-start | bytes 1671168 | tf_op jit(solution)/shard_map/all_gather | solution.py:140
  16.4 2.6 copy-start.3
  19.0 183.2 %copy-start.5 = (bf16[128,2880]{0,1:T(8,128)(2,1)}, bf16[128,2880]{0,1:T(8,128)(2,1)S(1)}, u32[]{:S(2)}) copy-start(bf16[128,2880]{0,1:T(8,128)(2,1)S(1)} %constant_dynamic-update-slice_fusion) | copy-start | bytes 2211844
  397.5 15.7 copy-start.7
  411.6 22.9 %copy-start.6 = (bf16[128,320]{0,1:T(8,128)(2,1)S(1)}, bf16[128,320]{0,1:T(8,128)(2,1)}, u32[]{:S(2)}) copy-start(bf16[128,320]{0,1:T(8,128)(2,1)} %get-tuple-element.317) | copy-start | bytes 245764
  438.1 0.9 copy-start.2
  463.3 396.9 %all-to-all-start = ((bf16[16,180,320]{2,1,0:T(8,128)(2,1)}), bf16[16,180,320]{2,1,0:T(8,128)(2,1)}, u32[]{:S(2)}, u32[]{:S(2)}) async-start(bf16[16,180,320]{2,1,0:T(8,128)(2,1)} %broadcast_select_fusion), calls=%async_computation | async-start | bytes 4521984 | tf_op jit(solution)/shard_map/all_to_all | solution.py:95
  477.3 1188.5 %all-reduce.7.cloned.1.call-start = ((), (), s32[]{:S(2)}) async-start(), calls=%async_computation.5 | async-start | bytes 1130496 | tf_op jit(solution)/shard_map/psum | solution.py:155
  860.2 2.9 copy-start.1
  860.2 2.9 copy-start.4
Sparse Core Ops, SparseCore 0:
  12.2 186.0 all-gather.12
  202.4 168.4 all-gather.10
  375.1 193.7 all-gather.6
  573.0 247.6 all-gather.8
  863.3 802.5 all-reduce.6
where the time goes:
time: 1680 us
  waiting for transfers between devices  1490 us (89%)
  local copies, waits for them, and re-layouts  102 us (6%)
  other arithmetic  35.3 us (2%)
    psum x1, waiting for transfers between devices, body(): second_total, first_total = lax.psum((second_owned, total), 'rep')  800 us
    all_gather x1, waiting for transfers between devices, body(): lax.all_gather(conv_grad.reshape(1, HEIGHT, WIDTH, C), 'dom', axis=0, til...  252 us
    all_gather x1, waiting for transfers between devices, body(): lax.all_gather(second_weight, 'dom', axis=0, tiled=True)  179 us
    all_gather x1, waiting for transfers between devices, body(): lax.all_gather(first_weight, 'dom', axis=0, tiled=True)  169 us
    all_gather x1, waiting for transfers between devices, body(): lax.all_gather(first_act.reshape(1, HEIGHT, WIDTH, C), 'dom', axis=0, til...  91.6 us
  transfers between devices with their start and end apart: 6, of which 5 were waited for; matrix products, arithmetic and copies ran while one was open for 9% of the time, Pallas kernels for 0%

commit v1 on v0

v1 whole, which is shorter than its diff:
```python
import math

import jax
import jax.numpy as jnp
from jax import lax
from jax.experimental import pallas as pl
from jax.experimental.pallas import tpu as pltpu
from jax.sharding import PartitionSpec as P

C = 320
TEMB = 1280
HEIGHT = 8
WIDTH = 16
PIX = HEIGHT * WIDTH
NX, NY, NZH, NZL = 4, 4, 4, 8
BLOCK = 180
QROWS = 45
SAMPLES = 1024
MESH = pl.DeviceIdType.MESH
norm_eps = 1e-05
bf16 = jnp.bfloat16
f32 = jnp.float32

VM = pl.BlockSpec(memory_space=pltpu.VMEM)
SM = pl.BlockSpec(memory_space=pltpu.SMEM)


def position():
    rep, dom = lax.axis_index("rep"), lax.axis_index("dom")
    return rep // 8, lax.rem(rep // 2, 4), lax.rem(rep, 2), dom // 4, lax.rem(dom, 4)


def device(z_lo, x, core, z_hi, y):
    return {"rep": z_lo * 8 + x * 2 + core, "dom": z_hi * 4 + y}


def greet(partners):
    barrier = pltpu.get_barrier_semaphore()
    for partner in partners:
        pl.semaphore_signal(barrier, inc=1, device_id=partner, device_id_type=MESH)
    pl.semaphore_wait(barrier, len(partners))


def send(src, dst, send_sem, recv_sem, target):
    copy = pltpu.make_async_remote_copy(
        src_ref=src, dst_ref=dst, send_sem=send_sem, recv_sem=recv_sem,
        device_id=target, device_id_type=MESH,
    )
    copy.start()
    return copy


def pack_block(w):
    fold = jnp.concatenate([w[:96, 256:], jnp.pad(w[96:, 256:], ((0, 12), (0, 0)))], axis=1)
    pad = ((0, 12), (0, 0))
    return jnp.concatenate(
        [jnp.pad(w[:, :128], pad), jnp.pad(w[:, 128:256], pad), fold, jnp.zeros((32, 128), w.dtype)],
        axis=0,
    ).reshape(4, 128, 128)


def weights_kernel(own_ref, out_ref, own_sem, zs, zr, so, ro, s2, r2, s3, r3, sc, rc):
    z_lo, x, core, z_hi, y = position()
    to_z = [device(z_lo, x, core, lax.rem(z_hi + d, 4), y) for d in (1, 2, 3)]
    to_x = [device(z_lo, lax.rem(x + d, 4), core, z_hi, y) for d in (1, 2, 3)]
    to_y = [device(z_lo, x, core, z_hi, lax.rem(y + d, 4)) for d in (1, 2, 3)]
    other = device(z_lo, x, 1 - core, z_hi, y)
    keep = [pltpu.make_async_copy(own_ref.at[k], out_ref.at[k, z_hi, y], own_sem.at[k]) for k in (0, 1)]
    for copy in keep:
        copy.start()
    greet(to_z + to_x + to_y + [other])

    def run(c):
        sent = []

        def go(*copy):
            sent.append(send(*copy))
            return sent[-1]

        def arrived(copies):
            for copy in copies:
                copy.wait_recv()

        def block(d):
            return lax.rem(z_hi + 4 - d, 4)

        zc = {d: go(own_ref.at[c, x], out_ref.at[c, z_hi, y, x], zs.at[d - 1], zr.at[d - 1], to_z[d - 1]) for d in (2, 1, 3)}
        oc = [go(own_ref.at[c], out_ref.at[c, z_hi, y], so.at[j], ro.at[j], to_y[j]) for j in (1, 0, 2)]
        near, far = (to_x, to_y) if c == 0 else (to_y, to_x)

        def second(d):
            arrived([zc[d]])
            part = out_ref.at[c, block(d), y, x]
            return [go(part, part, s2.at[d - 1, j], r2.at[d - 1, j], near[j]) for j in (1, 0, 2)]

        def third(d, before):
            arrived(before)
            if c == 0:
                part = out_ref.at[0, block(d), y]
                return [go(part, part, s3.at[d - 1, 0, j], r3.at[d - 1, 0, j], far[j]) for j in (1, 0, 2)]
            copies = []
            for i in range(4):
                part = out_ref.at[1, block(d), lax.rem(y + i, 4), x]
                copies += [go(part, part, s3.at[d - 1, i, j], r3.at[d - 1, i, j], far[j]) for j in (1, 0, 2)]
            return copies

        def fourth(d, before):
            arrived(before)
            part = out_ref.at[c, block(d)]
            return [go(part, part, sc.at[d], rc.at[d], other)]

        for copy in keep:
            copy.wait()
        a1 = second(1)
        a3 = second(3)
        b1 = third(1, a1)
        b3 = third(3, a3)
        arrived(oc)
        last = []
        for i in (1, 2, 3):
            part = out_ref.at[c, z_hi, lax.rem(y + i, 4)]
            last.append(go(part, part, sc.at[3 + i], rc.at[3 + i], other))
        a2 = second(2)
        last += fourth(1, b1)
        b2 = third(2, a2)
        last += fourth(3, b3)
        last += fourth(2, b2)
        arrived(last)
        for copy in sent:
            copy.wait_send()

    for c in (0, 1):
        pl.when(core == c)(lambda c=c: run(c))


def gather_weights(own):
    dma = pltpu.SemaphoreType.DMA
    return pl.pallas_call(
        weights_kernel,
        out_shape=jax.ShapeDtypeStruct((2, NZH, NY, 4, 128, 128), bf16),
        in_specs=[VM],
        out_specs=VM,
        scratch_shapes=[
            dma((2,)), dma((3,)), dma((3,)), dma((3,)), dma((3,)), dma((3, 3)), dma((3, 3)),
            dma((3, 4, 3)), dma((3, 4, 3)), dma((7,)), dma((7,)),
        ],
        compiler_params=pltpu.CompilerParams(collective_id=0, has_side_effects=True),
        name="weights",
    )(own)


def group_matrix():
    row = lax.broadcasted_iota(jnp.int32, (C, C), 0).astype(f32)
    col = lax.broadcasted_iota(jnp.int32, (C, C), 1).astype(f32)
    same = jnp.floor((row + 0.5) * 0.1) == jnp.floor((col + 0.5) * 0.1)
    return jnp.where(same, 1.0, 0.0).astype(f32)


def shifted(v, step, rows):
    if step == 0:
        return v
    column = lax.rem(lax.broadcasted_iota(jnp.int32, (rows, C), 0), WIDTH)
    inside = (column + step >= 0) & (column + step < WIDTH)
    return jnp.where(inside, pltpu.roll(v, (-step) % rows, 0), 0.0)


def sample_kernel(
    index_ref, x_ref, cot_ref, bias_ref, w_ref, out_ref, act1_ref, grad_ref, act2_ref,
    wl1, wl2, pad,
):
    member = group_matrix()
    count = 1.0 / (PIX * 10)

    def group_mean(v):
        column = jnp.sum(v, axis=0, keepdims=True)
        return jnp.dot(
            jnp.broadcast_to(column, (8, C)), member,
            precision=lax.Precision.HIGHEST, preferred_element_type=f32,
        )[0:1] * count

    def group_norm(v):
        centered = v - group_mean(v)
        inverse_std = lax.rsqrt(group_mean(centered * centered) + norm_eps)
        return centered * inverse_std, inverse_std

    for kernel, target in ((0, wl1), (1, wl2)):
        for j in range(16):
            v = w_ref[kernel, index_ref[j]]
            base = BLOCK * j
            target[base : base + 180, 0:128] = v[0:180]
            target[base : base + 180, 128:256] = v[192:372]
            target[base : base + 96, 256:320] = v[384:480, 0:64]
            target[base + 96 : base + 180, 256:320] = v[384:468, 64:128]

    pad[:, 0:16, :] = jnp.zeros((3, 16, C), bf16)
    pad[:, 144:160, :] = jnp.zeros((3, 16, C), bf16)

    def fill(v):
        for k in range(3):
            pad[k, 16:144, :] = shifted(v, k - 1, PIX).astype(bf16)

    def conv(weight):
        total = jnp.zeros((PIX, C), f32)
        for t in range(9):
            ky, kx = t // 3, t % 3
            total = total + jnp.dot(
                pad[kx, 16 * ky : 16 * ky + PIX, :], weight[C * t : C * t + C, :],
                preferred_element_type=f32,
            )
        return total

    source = x_ref[...].astype(f32)
    normed, _ = group_norm(source)
    first_act = (normed * (1.0 / (1.0 + jnp.exp(-normed)))).astype(bf16)
    act1_ref[...] = first_act
    fill(first_act.astype(f32))
    second_norm, second_std = group_norm(conv(wl1) + bias_ref[...])
    gate = 1.0 / (1.0 + jnp.exp(-second_norm))
    second_act = (second_norm * gate).astype(bf16)
    act2_ref[...] = second_act
    fill(second_act.astype(f32))
    out_ref[...] = (source + conv(wl2)).astype(bf16)
    fill(cot_ref[...].astype(f32))
    act_grad = jnp.zeros((PIX, C), f32)
    for t in range(9):
        ky, kx = 2 - t // 3, 2 - t % 3
        act_grad = act_grad + lax.dot_general(
            pad[kx, 16 * ky : 16 * ky + PIX, :], wl2[C * t : C * t + C, :],
            (((1,), (1,)), ((), ())), preferred_element_type=f32,
        )
    norm_grad = act_grad * gate * (1.0 + second_norm * (1.0 - gate))
    grad_ref[...] = (
        second_std
        * (norm_grad - group_mean(norm_grad) - second_norm * group_mean(norm_grad * second_norm))
    ).astype(bf16)


def run_sample(index, x, cot, bias, weights):
    row = jax.ShapeDtypeStruct((PIX, C), bf16)
    return pl.pallas_call(
        sample_kernel,
        out_shape=(row, row, row, row),
        in_specs=[SM, VM, VM, VM, VM],
        out_specs=(VM, VM, VM, VM),
        scratch_shapes=[
            pltpu.VMEM((9 * C, C), bf16), pltpu.VMEM((9 * C, C), bf16), pltpu.VMEM((3, 160, C), bf16),
        ],
        name="sample",
    )(index, x, cot, bias, weights)


def exchange_kernel(act1_ref, grad_ref, act2_ref, cot_ref, acts_ref, grads_ref, own_sem, ss, rs):
    z_lo, x, core, z_hi, y = position()
    slot = x * 2 + core
    partners = [device(z_lo, x, 1 - core, z_hi, y)]
    for d in (1, 2, 3):
        for c in (0, 1):
            partners.append(device(z_lo, lax.rem(x + d, 4), c, z_hi, y))
    greet(partners)
    pairs = ((act1_ref, grad_ref), (act2_ref, cot_ref))
    outs = (acts_ref, grads_ref)
    for c in (0, 1):
        @pl.when(core == c)
        def _():
            mine = [pltpu.make_async_copy(pairs[c][a], outs[a].at[slot], own_sem.at[a]) for a in (0, 1)]
            for m in mine:
                m.start()
            copies = []
            for d in (2, 1, 3):
                for to in (0, 1):
                    for a in (0, 1):
                        copies.append(
                            send(pairs[to][a], outs[a].at[slot], ss.at[d, to, a], rs.at[d, c, a],
                                 partners[1 + (d - 1) * 2 + to])
                        )
            for a in (0, 1):
                copies.append(
                    send(pairs[1 - c][a], outs[a].at[slot], ss.at[0, 1 - c, a], rs.at[0, c, a], partners[0])
                )
            for m in mine:
                m.wait()
            for copy in copies:
                copy.wait_send()
            for d in (1, 2, 3):
                for source in (0, 1):
                    for a in (0, 1):
                        pltpu.make_async_copy(outs[a].at[slot], outs[a].at[slot], rs.at[d, source, a]).wait()
            for a in (0, 1):
                pltpu.make_async_copy(outs[a].at[slot], outs[a].at[slot], rs.at[0, 1 - c, a]).wait()


def exchange(act1, grad, act2, cot):
    dma = pltpu.SemaphoreType.DMA
    eight = jax.ShapeDtypeStruct((8, PIX, C), bf16)
    return pl.pallas_call(
        exchange_kernel,
        out_shape=(eight, eight),
        in_specs=[VM] * 4,
        out_specs=(VM, VM),
        scratch_shapes=[dma((2,)), dma((4, 2, 2)), dma((4, 2, 2))],
        compiler_params=pltpu.CompilerParams(collective_id=1, has_side_effects=True),
        name="exchange",
    )(act1, grad, act2, cot)


def gradient_kernel(start_ref, act_ref, grad_ref, out_ref, act_t, pad, total):
    for s in range(8):
        act_t[:, PIX * s : PIX * s + PIX] = act_ref[s].astype(f32).T.astype(bf16)
        pad[:, s, 0:16, :] = jnp.zeros((3, 16, C), bf16)
        pad[:, s, 144:160, :] = jnp.zeros((3, 16, C), bf16)
        v = grad_ref[s].astype(f32)
        for k in range(3):
            pad[k, s, 16:144, :] = shifted(v, k - 1, PIX).astype(bf16)
    total[9 * C :, :] = jnp.zeros((24, C), f32)

    @pl.loop(0, 9)
    def _(t):
        ky, kx = 2 - t // 3, 2 - lax.rem(t, 3)
        rows = pad[kx, :, pl.ds(pl.multiple_of(16 * ky, 16), PIX), :].reshape(8 * PIX, C)
        total[pl.ds(pl.multiple_of(C * t, 8), C), :] = jnp.dot(
            act_t[...], rows, preferred_element_type=f32
        )

    for d in range(16):
        first = start_ref[d]
        base = pl.multiple_of((first // 8) * 8, 8)
        v = pltpu.roll(total[pl.ds(base, 56), :], 56 - lax.rem(first, 8), 0)
        fold = jnp.concatenate([v[0:24, 256:320], v[24:48, 256:320]], axis=1)
        tile = jnp.concatenate([v[0:48, 0:128], v[0:48, 128:256], fold, jnp.zeros((8, 128), f32)], axis=0)
        out_ref[d % 4, d // 4] = tile.astype(bf16).reshape(NZL, 16, 128)


def run_gradient(starts, acts, grads):
    return pl.pallas_call(
        gradient_kernel,
        out_shape=jax.ShapeDtypeStruct((NY, NZH, NZL, 16, 128), bf16),
        in_specs=[SM, VM, VM],
        out_specs=VM,
        scratch_shapes=[
            pltpu.VMEM((C, 8 * PIX), bf16), pltpu.VMEM((3, 8, 160, C), bf16), pltpu.VMEM((9 * C + 24, C), f32),
        ],
        name="gradient",
    )(starts, acts, grads)


def reduce_kernel(
    part_ref, first_ref, second_ref, ybuf, s1, zbuf, s2, hbuf, final, all_ref,
    ys, yr, ls, lr, hs, hr, gs, gr, xs, xr, cs, cr, own_sem,
):
    z_lo, x, core, z_hi, y = position()
    to_y = [device(z_lo, x, core, z_hi, lax.rem(y + d, 4)) for d in (1, 2, 3)]
    to_l = [device(lax.rem(z_lo + d, 8), x, core, z_hi, y) for d in range(1, 8)]
    to_h = [device(z_lo, x, core, lax.rem(z_hi + d, 4), y) for d in (1, 2, 3)]
    to_x = [device(z_lo, lax.rem(x + d, 4), core, z_hi, y) for d in (1, 2, 3)]
    other = device(z_lo, x, 1 - core, z_hi, y)
    greet(to_y + to_l + to_h + to_x + [other])

    copies = [
        send(part_ref.at[lax.rem(y + d, 4)], ybuf.at[d - 1], ys.at[d - 1], yr.at[d - 1], to_y[d - 1])
        for d in (2, 1, 3)
    ]
    for c in copies:
        c.wait()
    for e in range(NZH):
        total = part_ref[y, e].astype(f32)
        for d in range(3):
            total = total + ybuf[d, e].astype(f32)
        s1[:, e] = total.astype(bf16)

    copies = [
        send(s1.at[lax.rem(z_lo + d, 8)], zbuf.at[d - 1], ls.at[d - 1], lr.at[d - 1], to_l[d - 1])
        for d in (4, 3, 5, 2, 6, 1, 7)
    ]
    for c in copies:
        c.wait()
    total = s1[z_lo].astype(f32)
    for d in range(7):
        total = total + zbuf[d].astype(f32)
    s2[...] = total.astype(bf16)

    copies = [
        send(s2.at[lax.rem(z_hi + d, 4)], hbuf.at[d - 1], hs.at[d - 1], hr.at[d - 1], to_h[d - 1])
        for d in (2, 1, 3)
    ]
    for c in copies:
        c.wait()
    total = s2[z_hi].astype(f32)
    for d in range(3):
        total = total + hbuf[d].astype(f32)
    final[...] = total * (1.0 / SAMPLES)

    keep = pltpu.make_async_copy(final, all_ref.at[core, x, z_lo], own_sem)
    keep.start()
    copies = [
        send(final, all_ref.at[core, x, z_lo], gs.at[d - 1], gr.at[d - 1], to_l[d - 1])
        for d in (4, 3, 5, 2, 6, 1, 7)
    ]
    keep.wait()
    for c in copies:
        c.wait()
    quarter = all_ref.at[core, x]
    copies = [send(quarter, quarter, xs.at[d - 1], xr.at[d - 1], to_x[d - 1]) for d in (2, 1, 3)]
    for c in copies:
        c.wait()
    whole = all_ref.at[core]
    send(whole, whole, cs, cr, other).wait()

    for kernel, target in ((0, first_ref), (1, second_ref)):
        for q in range(4):
            v = all_ref[kernel, q].reshape(128, 128)
            base = QROWS * q
            target[base : base + 45, 0:128] = v[0:45]
            target[base : base + 45, 128:256] = v[48:93]
            target[base : base + 24, 256:320] = v[96:120, 0:64]
            target[base + 24 : base + 45, 256:320] = v[96:117, 64:128]


def reduce_all(part):
    dma = pltpu.SemaphoreType.DMA
    out = jax.ShapeDtypeStruct((BLOCK, C), f32)
    return pl.pallas_call(
        reduce_kernel,
        out_shape=(out, out),
        in_specs=[VM],
        out_specs=(VM, VM),
        scratch_shapes=[
            pltpu.VMEM((3, NZH, NZL, 16, 128), bf16),
            pltpu.VMEM((NZL, NZH, 16, 128), bf16),
            pltpu.VMEM((7, NZH, 16, 128), bf16),
            pltpu.VMEM((NZH, 16, 128), bf16),
            pltpu.VMEM((3, 16, 128), bf16),
            pltpu.VMEM((16, 128), f32),
            pltpu.VMEM((2, NX, NZL, 16, 128), f32),
            dma((3,)), dma((3,)), dma((7,)), dma((7,)), dma((3,)), dma((3,)),
            dma((7,)), dma((7,)), dma((3,)), dma((3,)), dma, dma, dma,
        ],
        compiler_params=pltpu.CompilerParams(collective_id=2, has_side_effects=True),
        name="reduce",
    )(part)


def time_bias(timestep, time_weight):
    half_dim = TEMB // 2
    frequency = jnp.exp(-math.log(10000.0) * jnp.arange(half_dim, dtype=f32) / half_dim)
    angles = timestep.astype(f32) * frequency
    embedded = jnp.concatenate([jnp.cos(angles), jnp.sin(angles)])
    activated = jax.nn.silu(embedded).astype(bf16)
    return jnp.dot(activated[None, :], time_weight, preferred_element_type=f32)


def body(block_input, cotangent, timesteps, owner_map, time_weight, first_weight, second_weight):
    own = jnp.stack([pack_block(first_weight), pack_block(second_weight)])
    ids = jnp.arange(16, dtype=jnp.int32)
    inverse = jnp.sum((owner_map[None, :] == ids[:, None]).astype(jnp.int32) * ids[None, :], axis=1)
    quarter = lax.rem(lax.axis_index("rep") // 2, 4)
    starts = inverse * BLOCK + quarter.astype(jnp.int32) * QROWS
    bias = time_bias(timesteps[0], time_weight)
    weights = gather_weights(own).reshape(2, 16, 512, 128)
    x = block_input.reshape(PIX, C)
    cot = cotangent.reshape(PIX, C)
    out, act1, grad, act2 = run_sample(owner_map, x, cot, bias, weights)
    acts, grads = exchange(act1, grad, act2, cot)
    part = run_gradient(starts, acts, grads)
    first_grad, second_grad = reduce_all(part)
    return out.reshape(1, HEIGHT, WIDTH, C), first_grad, second_grad


def solution(mesh):
    placed = (
        P(("rep", "dom"), None, None, None),
        P(("rep", "dom"), None, None, None),
        P(("rep", "dom")),
        P(),
        P(),
        P("dom", None),
        P("dom", None),
    )
    return jax.shard_map(
        body,
        mesh=mesh,
        in_specs=placed,
        out_specs=(P(("rep", "dom"), None, None, None), P("dom", None), P("dom", None)),
        check_vma=False,
    )
```

time: 1680 us -> 170 us (0.10)
  waiting for transfers between devices: 1490 us -> 0 us
  Pallas kernels: 0 us -> 158 us
  local copies, waits for them, and re-layouts: 102 us -> 7.37 us
  other arithmetic: 35.3 us -> 1.58 us
    psum x1 -> x0, waiting for transfers between devices: 800 us -> none  [body(): second_total, first_total = lax.psum((second_owned, total), 'rep')]
    all_gather x4 -> x0, waiting for transfers between devices: 691 us -> none  [the longest x1 252 us: body(): lax.all_gather(conv_grad.reshape(1, HEIGHT, WIDTH, C), 'dom', axis=0, til...]
    pallas_call x0 -> x5, Pallas kernels: none -> 158 us  [the longest x1 63.2 us: gather_weights(): pl.pallas_call(weights_kernel, out_shape=jax.ShapeDtypeStruct((2, NZH, NY...]
    reshape x5 -> x0, local copies, waits for them, and re-layouts: 22.7 us -> none  [the longest x2 14.1 us: second_owner_sum(): term_rounded.reshape(group_size, block_rows, C)]
    dynamic_slice x33 -> x0, local copies, waits for them, and re-layouts: 17.1 us -> none  [the longest x16 14.5 us: body(): lax.scan(add_one, jnp.zeros((block_rows, C), jnp.float32), (act_piece, gr...]
  transfers between devices with their start and end apart: 6 -> 0, of which waited for: 5 -> 0; matrix products, arithmetic and copies ran while one was open for 9% -> 0% of each run, Pallas kernels for 0% -> 0%
where the time goes in v1:
time: 170 us; the launch traced here: 169 us
  Pallas kernels  158 us (93%)
  local copies, waits for them, and re-layouts  7.37 us (4%)
    pallas_call x1, Pallas kernels, gather_weights(): pl.pallas_call(weights_kernel, out_shape=jax.ShapeDtypeStruct((2, NZH, NY...  63.2 us
    pallas_call x1, Pallas kernels, reduce_all(): pl.pallas_call(reduce_kernel, out_shape=(out, out), in_specs=[VM], out_sp...  54.1 us
    pallas_call x1, Pallas kernels, exchange(): pl.pallas_call(exchange_kernel, out_shape=(eight, eight), in_specs=[VM] *...  24.1 us
    pallas_call x1, Pallas kernels, run_gradient(): pl.pallas_call(gradient_kernel, out_shape=jax.ShapeDtypeStruct((NY, NZH,...  8.17 us
    pallas_call x1, Pallas kernels, run_sample(): pl.pallas_call(sample_kernel, out_shape=(row, row, row, row), in_specs=[S...  8.02 us

profile of v1, /device:TPU:1, one launch (start us, length us, event | category | flops | bytes accessed | tf_op | source)
XLA Modules:
  0.0 168.9 jit_solution(16762716662938571334)
XLA Ops:
  0.6 0.0 copy-start
  0.6 1.0 fusion.21
  1.6 0.7 slice.26
  2.3 0.7 slice.30
  3.1 0.7 slice.27
  3.8 0.7 slice.31
  4.6 0.1 pad.37.clone
  4.6 0.1 fusion.12
  4.8 0.7 pad_maximum_fusion.own_ref
  5.5 0.0 copy-start.1
  5.5 63.2 %weights.1 = bf16[2,4,4,4,128,128]{5,4,3,2,1,0:T(8,128)(2,1)} custom-call(bf16[2,4,128,128]{3,2,1,0:T(8,128)(2,1)} %pad_maximum_fusion.own_ref), custom_call_target="tpu_custom_call" | custom-call | tf_op jit(solution)/shard_map/weights/pallas_call | solution.py:138
  69.4 0.0 copy-done
  69.5 0.9 fusion.23.bias_ref
  70.4 8.0 %sample.1 = (bf16[128,320]{1,0:T(8,128)(2,1)}, bf16[128,320]{1,0:T(8,128)(2,1)}, bf16[128,320]{1,0:T(8,128)(2,1)}, bf16[128,320]{1,0:T(8,128)(2,1)}) custom-call(s32[16]{0:T(128)} %index_ref.1, bf16[128,320]{1,0:T(8,128)(2,1)} %bitcast.14, bf16[128,320]{1,0:T(8,128)(2,1)} %bitcast.12, f32[1,320]{1,0:T(1,128)} %fusion.23.bias_ref, ...), custom_call_target="tpu_custom_call" | custom-call | tf_op jit(solution)/shard_map/sample/pallas_call | solution.py:240
  78.4 24.1 %exchange.1 = (bf16[8,128,320]{2,1,0:T(8,128)(2,1)}, bf16[8,128,320]{2,1,0:T(8,128)(2,1)}) custom-call(bf16[128,320]{1,0:T(8,128)(2,1)} %get-tuple-element.12.act1_ref, bf16[128,320]{1,0:T(8,128)(2,1)} %get-tuple-element.13.grad_ref, bf16[128,320]{1,0:T(8,128)(2,1)} %get-tuple-element.14.act2_ref, bf16[128,320]{1,0:T(8,128)(2,1)} %bitcast.13), custom_call_target="tpu_custom_call" | custom-call | tf_op jit(solution)/shard_map/exchange/pallas_call | solution.py:295
  102.5 0.0 copy-done.1
  102.5 0.1 select_reduce_fusion
  102.6 0.5 multiply_add_fusion.start_ref
  103.2 8.2 %gradient.1.part_ref = bf16[4,4,8,16,128]{4,3,2,1,0:T(8,128)(2,1)} custom-call(s32[16]{0:T(128)} %multiply_add_fusion.start_ref, bf16[8,128,320]{2,1,0:T(8,128)(2,1)} %get-tuple-element.15.act_ref, bf16[8,128,320]{2,1,0:T(8,128)(2,1)} %get-tuple-element.16.grad_ref), custom_call_target="tpu_custom_call" | custom-call | tf_op jit(solution)/shard_map/gradient/pallas_call | solution.py:334
  111.3 54.1 %reduce.1 = (f32[180,320]{1,0:T(8,128)}, f32[180,320]{1,0:T(8,128)}) custom-call(bf16[4,4,8,16,128]{4,3,2,1,0:T(8,128)(2,1)} %gradient.1.part_ref), custom_call_target="tpu_custom_call" | custom-call | tf_op jit(solution)/shard_map/reduce/pallas_call | solution.py:421
  165.5 1.7 copy.13
  167.2 1.7 copy.14
  (4 shorter events, 0.1 us)
Async XLA Ops:
  0.6 68.8 %copy-start = (bf16[1280,320]{0,1:T(8,128)(2,1)S(1)}, bf16[1280,320]{0,1:T(8,128)(2,1)}, u32[]{:S(2)}) copy-start(bf16[1280,320]{0,1:T(8,128)(2,1)} %param.11) | copy-start | bytes 2457604
  5.5 97.0 %copy-start.1 = (s32[16]{0:T(128)S(1)}, s32[16]{0:T(128)}, u32[]{:S(2)}) copy-start(s32[16]{0:T(128)} %index_ref.1) | copy-start | bytes 196

commit v2 on v0

v2 whole, which is shorter than its diff:
```python
import math

import jax
import jax.numpy as jnp
from jax import lax
from jax.experimental import pallas as pl
from jax.experimental.pallas import tpu as pltpu
from jax.sharding import PartitionSpec as P

C = 320
TEMB = 1280
HEIGHT = 8
WIDTH = 16
PIX = HEIGHT * WIDTH
NX, NY, NZH, NZL = 4, 4, 4, 8
BLOCK = 180
QROWS = 48
SAMPLES = 1024
MESH = pl.DeviceIdType.MESH
norm_eps = 1e-05
bf16 = jnp.bfloat16
f32 = jnp.float32

VM = pl.BlockSpec(memory_space=pltpu.VMEM)
SM = pl.BlockSpec(memory_space=pltpu.SMEM)


def position():
    rep, dom = lax.axis_index("rep"), lax.axis_index("dom")
    return rep // 8, lax.rem(rep // 2, 4), lax.rem(rep, 2), dom // 4, lax.rem(dom, 4)


def device(z_lo, x, core, z_hi, y):
    return {"rep": z_lo * 8 + x * 2 + core, "dom": z_hi * 4 + y}


def send(src, dst, send_sem, recv_sem, target):
    copy = pltpu.make_async_remote_copy(
        src_ref=src, dst_ref=dst, send_sem=send_sem, recv_sem=recv_sem,
        device_id=target, device_id_type=MESH,
    )
    copy.start()
    return copy


def group_matrix():
    row = lax.broadcasted_iota(jnp.int32, (C, C), 0).astype(f32)
    col = lax.broadcasted_iota(jnp.int32, (C, C), 1).astype(f32)
    same = jnp.floor((row + 0.5) * 0.1) == jnp.floor((col + 0.5) * 0.1)
    return jnp.where(same, 1.0, 0.0).astype(f32)


def shifted(v, step, rows):
    if step == 0:
        return v
    column = lax.rem(lax.broadcasted_iota(jnp.int32, (rows, C), 0), WIDTH)
    inside = (column + step >= 0) & (column + step < WIDTH)
    return jnp.where(inside, pltpu.roll(v, (-step) % rows, 0), 0.0)


def pack_block(w):
    w = w.astype(f32)
    pad = jnp.zeros((12, 128), f32)
    fold = jnp.concatenate(
        [w[0:96, 256:320], jnp.concatenate([w[96:180, 256:320], jnp.zeros((12, 64), f32)], axis=0)], axis=1
    )
    tiles = jnp.concatenate([w[:, 0:128], pad, w[:, 128:256], pad, fold, jnp.zeros((32, 128), f32)], axis=0)
    return tiles.astype(bf16).reshape(4, 128, 128)


def gather_weights(c, own, wg, keep, other, to_z, to_x, to_y, place, extra, zs, zr, so, ro, s2, r2, s3, r3, sc, rc):
    x, z_hi, y = place
    sent = []

    def go(*copy):
        sent.append(send(*copy))
        return sent[-1]

    def arrived(copies):
        for copy in copies:
            copy.wait_recv()

    def block(d):
        return lax.rem(z_hi + 4 - d, 4)

    zc = {
        d: go(own.at[c, x], wg.at[c, z_hi * 4 + y, x], zs.at[d - 1], zr.at[d - 1], to_z[d - 1])
        for d in (2, 1, 3)
    }
    oc = [go(own.at[c], wg.at[c, z_hi * 4 + y], so.at[j], ro.at[j], to_y[j]) for j in (1, 0, 2)]
    extra(go)
    near, far = (to_x, to_y) if c == 0 else (to_y, to_x)

    def second(d):
        arrived([zc[d]])
        part = wg.at[c, block(d) * 4 + y, x]
        return [go(part, part, s2.at[d - 1, j], r2.at[d - 1, j], near[j]) for j in (1, 0, 2)]

    def third(d, before):
        arrived(before)
        if c == 0:
            part = wg.at[0, block(d) * 4 + y]
            return [go(part, part, s3.at[d - 1, 0, j], r3.at[d - 1, 0, j], far[j]) for j in (1, 0, 2)]
        copies = []
        for i in range(4):
            part = wg.at[1, block(d) * 4 + lax.rem(y + i, 4), x]
            copies += [go(part, part, s3.at[d - 1, i, j], r3.at[d - 1, i, j], far[j]) for j in (1, 0, 2)]
        return copies

    def fourth(d, before):
        arrived(before)
        part = wg.at[c, pl.ds(block(d) * 4, 4)]
        return [go(part, part, sc.at[d], rc.at[d], other)]

    for copy in keep:
        copy.wait()
    a1 = second(1)
    a3 = second(3)
    b1 = third(1, a1)
    b3 = third(3, a3)
    arrived(oc)
    last = []
    for i in (1, 2, 3):
        part = wg.at[c, z_hi * 4 + lax.rem(y + i, 4)]
        last.append(go(part, part, sc.at[3 + i], rc.at[3 + i], other))
    a2 = second(2)
    last += fourth(1, b1)
    b2 = third(2, a2)
    last += fourth(3, b3)
    last += fourth(2, b2)
    arrived(last)
    for copy in sent:
        copy.wait_send()


def step_kernel(
    index_ref, tile_ref, odd_ref, x_ref, cot_ref, bias_ref, w1_ref, w2_ref,
    out_ref, all_ref,
    own, wg, wl1, wl2, pad, act1, act2, cgrad, acts, grads, act_t, pads, total,
    part_ref, ybuf, s1, zbuf, s2b, hbuf, final,
    own_sem, zs, zr, so, ro, s2, r2, s3, r3, sc, rc, sa, ra,
    ys, yr, ls, lr, hs, hr, gs, gr, xs, xr, cs, cr, keep_sem,
):
    z_lo, x, core, z_hi, y = position()
    slot = x * 2 + core
    to_z = [device(z_lo, x, core, lax.rem(z_hi + d, 4), y) for d in (1, 2, 3)]
    to_y = [device(z_lo, x, core, z_hi, lax.rem(y + d, 4)) for d in (1, 2, 3)]
    to_l = [device(lax.rem(z_lo + d, 8), x, core, z_hi, y) for d in range(1, 8)]
    at_x = [[device(z_lo, lax.rem(x + d, 4), c, z_hi, y) for d in (1, 2, 3)] for c in (0, 1)]
    to_x = [device(z_lo, lax.rem(x + d, 4), core, z_hi, y) for d in (1, 2, 3)]
    other = device(z_lo, x, 1 - core, z_hi, y)
    partners = to_z + to_y + to_l + at_x[0] + at_x[1] + [other]
    barrier = pltpu.get_barrier_semaphore()
    for partner in partners:
        pl.semaphore_signal(barrier, inc=1, device_id=partner, device_id_type=MESH)

    member = group_matrix()
    count = 1.0 / (PIX * 10)

    def group_mean(v):
        column = jnp.sum(v, axis=0, keepdims=True)
        return jnp.dot(
            jnp.broadcast_to(column, (8, C)), member,
            precision=lax.Precision.HIGHEST, preferred_element_type=f32,
        )[0:1] * count

    def group_norm(v):
        centered = v - group_mean(v)
        inverse_std = lax.rsqrt(group_mean(centered * centered) + norm_eps)
        return centered * inverse_std, inverse_std

    own[0] = pack_block(w1_ref[...])
    own[1] = pack_block(w2_ref[...])
    source = x_ref[...].astype(f32)
    normed, _ = group_norm(source)
    act1[...] = (normed * (1.0 / (1.0 + jnp.exp(-normed)))).astype(bf16)
    pad[:, 0:16, :] = jnp.zeros((3, 16, C), bf16)
    pad[:, 144:160, :] = jnp.zeros((3, 16, C), bf16)
    pads[:, :, 0:16, :] = jnp.zeros((3, 8, 16, C), bf16)
    pads[:, :, 144:160, :] = jnp.zeros((3, 8, 16, C), bf16)
    total[9 * C // 8 :] = jnp.zeros((3, 8, C), f32)

    def fill(v):
        for k in range(3):
            pad[k, 16:144, :] = shifted(v, k - 1, PIX).astype(bf16)

    fill(act1[...].astype(f32))

    @pl.when(core == 0)
    def _():
        acts[slot] = act1[...]

    @pl.when(core == 1)
    def _():
        grads[slot] = cot_ref[...]

    pl.semaphore_wait(barrier, len(partners))

    keep = [pltpu.make_async_copy(own.at[k], wg.at[k, z_hi * 4 + y], own_sem.at[k]) for k in (0, 1)]
    for copy in keep:
        copy.start()

    for c in (0, 1):

        def run(c=c):
            def extra(go):
                for j in (1, 0, 2):
                    go(act1, acts.at[slot], sa.at[0, j + 1], ra.at[0, j + 1, c], at_x[0][j])
                    go(cot_ref, grads.at[slot], sa.at[2, j + 1], ra.at[1, j + 1, c], at_x[1][j])
                if c == 1:
                    go(act1, acts.at[slot], sa.at[0, 0], ra.at[0, 0, 1], other)
                else:
                    go(cot_ref, grads.at[slot], sa.at[2, 0], ra.at[1, 0, 0], other)

            gather_weights(
                c, own, wg, keep, other, to_z, to_x, to_y, (x, z_hi, y), extra,
                zs, zr, so, ro, s2, r2, s3, r3, sc, rc,
            )

        pl.when(core == c)(run)

    for kernel, target in ((0, wl1), (1, wl2)):
        for j in range(16):
            v = wg[kernel, index_ref[j]].reshape(512, 128)
            base = BLOCK * j
            target[base : base + 180, 0:128] = v[0:180]
            target[base : base + 180, 128:256] = v[192:372]
            target[base : base + 96, 256:320] = v[384:480, 0:64]
            target[base + 96 : base + 180, 256:320] = v[384:468, 64:128]

    def conv(weight):
        result = jnp.zeros((PIX, C), f32)
        for t in range(9):
            ky, kx = t // 3, t % 3
            result = result + jnp.dot(
                pad[kx, 16 * ky : 16 * ky + PIX, :], weight[C * t : C * t + C, :],
                preferred_element_type=f32,
            )
        return result

    second_norm, second_std = group_norm(conv(wl1) + bias_ref[...])
    gate = 1.0 / (1.0 + jnp.exp(-second_norm))
    second_act = (second_norm * gate).astype(bf16)
    act2[...] = second_act

    @pl.when(core == 1)
    def _():
        acts[slot] = act2[...]

    fill(cot_ref[...].astype(f32))
    sent = [
        send(act2, acts.at[slot], sa.at[1, j + 1], ra.at[0, j + 1, core], at_x[1][j]) for j in (1, 0, 2)
    ]

    @pl.when(core == 0)
    def _():
        send(act2, acts.at[slot], sa.at[1, 0], ra.at[0, 0, 0], other)

    act_grad = jnp.zeros((PIX, C), f32)
    for t in range(9):
        ky, kx = 2 - t // 3, 2 - t % 3
        act_grad = act_grad + lax.dot_general(
            pad[kx, 16 * ky : 16 * ky + PIX, :], wl2[C * t : C * t + C, :],
            (((1,), (1,)), ((), ())), preferred_element_type=f32,
        )
    norm_grad = act_grad * gate * (1.0 + second_norm * (1.0 - gate))
    cgrad[...] = (
        second_std
        * (norm_grad - group_mean(norm_grad) - second_norm * group_mean(norm_grad * second_norm))
    ).astype(bf16)

    @pl.when(core == 0)
    def _():
        grads[slot] = cgrad[...]

    sent += [
        send(cgrad, grads.at[slot], sa.at[3, j + 1], ra.at[1, j + 1, core], at_x[0][j]) for j in (1, 0, 2)
    ]

    @pl.when(core == 1)
    def _():
        send(cgrad, grads.at[slot], sa.at[3, 0], ra.at[1, 0, 1], other)

    fill(act2[...].astype(f32))
    out_ref[...] = (x_ref[...].astype(f32) + conv(wl2)).astype(bf16)

    def take_acts():
        for d in (1, 2, 3):
            for c in (0, 1):
                pltpu.make_async_copy(acts.at[slot], acts.at[slot], ra.at[0, d, c]).wait()
        pltpu.make_async_copy(acts.at[slot], acts.at[slot], ra.at[0, 0, 1 - core]).wait()

        @pl.loop(0, 8)
        def _(s):
            act_t[:, pl.ds(pl.multiple_of(PIX * s, PIX), PIX)] = acts[s].astype(f32).T.astype(bf16)

    def take_grads():
        for d in (1, 2, 3):
            for c in (0, 1):
                pltpu.make_async_copy(grads.at[slot], grads.at[slot], ra.at[1, d, c]).wait()
        pltpu.make_async_copy(grads.at[slot], grads.at[slot], ra.at[1, 0, 1 - core]).wait()

        @pl.loop(0, 8)
        def _(s):
            v = grads[s].astype(f32)
            for k in range(3):
                pads[k, s, 16:144, :] = shifted(v, k - 1, PIX).astype(bf16)

    @pl.when(core == 0)
    def _():
        take_acts()
        take_grads()
        pltpu.make_async_copy(act2, acts.at[slot], sa.at[1, 0]).wait()

    @pl.when(core == 1)
    def _():
        take_grads()
        take_acts()
        pltpu.make_async_copy(cgrad, grads.at[slot], sa.at[3, 0]).wait()

    for copy in sent:
        copy.wait_send()

    @pl.loop(0, 9)
    def _(t):
        ky, kx = 2 - t // 3, 2 - lax.rem(t, 3)
        rows = pads[kx, :, pl.ds(pl.multiple_of(16 * ky, 16), PIX), :].reshape(8 * PIX, C)
        product = jnp.dot(act_t[...], rows, preferred_element_type=f32)
        total[pl.ds((C // 8) * t, C // 8)] = product.reshape(C // 8, 8, C)

    ycopies = []
    for d in (2, 1, 3, 0):
        column = lax.rem(y + d, 4)
        for e in range(4):
            first = tile_ref[e * 4 + column]
            v = jnp.concatenate([total[first + i] for i in range(7)], axis=0)
            late = jnp.full((48, C), odd_ref[e * 4 + column], jnp.int32) > 0
            v = jnp.where(late, v[4:52], v[0:48])
            fold = jnp.concatenate([v[0:24, 256:320], v[24:48, 256:320]], axis=1)
            tile = jnp.concatenate([v[0:48, 0:128], v[0:48, 128:256], fold, jnp.zeros((8, 128), f32)], axis=0)
            part_ref[column, e] = tile.astype(bf16).reshape(NZL, 16, 128)
        if d > 0:
            ycopies.append(
                send(part_ref.at[column], ybuf.at[d - 1], ys.at[d - 1], yr.at[d - 1], to_y[d - 1])
            )
    for c in ycopies:
        c.wait()
    for e in range(NZH):
        v = part_ref[y, e].astype(f32)
        for d in range(3):
            v = v + ybuf[d, e].astype(f32)
        s1[:, e] = v.astype(bf16)

    copies = [
        send(s1.at[lax.rem(z_lo + d, 8)], zbuf.at[d - 1], ls.at[d - 1], lr.at[d - 1], to_l[d - 1])
        for d in (4, 3, 5, 2, 6, 1, 7)
    ]
    for c in copies:
        c.wait()
    v = s1[z_lo].astype(f32)
    for d in range(7):
        v = v + zbuf[d].astype(f32)
    s2b[...] = v.astype(bf16)

    copies = [
        send(s2b.at[lax.rem(z_hi + d, 4)], hbuf.at[d - 1], hs.at[d - 1], hr.at[d - 1], to_z[d - 1])
        for d in (2, 1, 3)
    ]
    for c in copies:
        c.wait()
    v = s2b[z_hi].astype(f32)
    for d in range(3):
        v = v + hbuf[d].astype(f32)
    final[...] = (v * (1.0 / SAMPLES)).astype(bf16)

    kept = pltpu.make_async_copy(final, all_ref.at[core, x, z_lo], keep_sem)
    kept.start()
    copies = [
        send(final, all_ref.at[core, x, z_lo], gs.at[d - 1], gr.at[d - 1], to_l[d - 1])
        for d in (4, 3, 5, 2, 6, 1, 7)
    ]
    kept.wait()
    for c in copies:
        c.wait()
    quarter = all_ref.at[core, x]
    copies = [send(quarter, quarter, xs.at[d - 1], xr.at[d - 1], to_x[d - 1]) for d in (2, 1, 3)]
    for c in copies:
        c.wait()
    whole = all_ref.at[core]
    send(whole, whole, cs, cr, other).wait()


def run_step(index, tiles, odd, x, cot, bias, first_weight, second_weight):
    dma = pltpu.SemaphoreType.DMA
    v = pltpu.VMEM
    return pl.pallas_call(
        step_kernel,
        out_shape=(
            jax.ShapeDtypeStruct((PIX, C), bf16),
            jax.ShapeDtypeStruct((2, NX, NZL, 16, 128), bf16),
        ),
        in_specs=[SM, SM, SM, VM, VM, VM, VM, VM],
        out_specs=(VM, VM),
        scratch_shapes=[
            v((2, 4, 128, 128), bf16), v((2, NZH * NY, 4, 128, 128), bf16),
            v((9 * C, C), bf16), v((9 * C, C), bf16), v((3, 160, C), bf16),
            v((PIX, C), bf16), v((PIX, C), bf16), v((PIX, C), bf16),
            v((8, PIX, C), bf16), v((8, PIX, C), bf16), v((C, 8 * PIX), bf16),
            v((3, 8, 160, C), bf16), v((9 * C // 8 + 3, 8, C), f32),
            v((NY, NZH, NZL, 16, 128), bf16), v((3, NZH, NZL, 16, 128), bf16),
            v((NZL, NZH, 16, 128), bf16), v((7, NZH, 16, 128), bf16), v((NZH, 16, 128), bf16),
            v((3, 16, 128), bf16), v((16, 128), bf16),
            dma((2,)), dma((3,)), dma((3,)), dma((3,)), dma((3,)), dma((3, 3)), dma((3, 3)),
            dma((3, 4, 3)), dma((3, 4, 3)), dma((7,)), dma((7,)), dma((4, 4)), dma((2, 4, 2)),
            dma((3,)), dma((3,)), dma((7,)), dma((7,)), dma((3,)), dma((3,)),
            dma((7,)), dma((7,)), dma((3,)), dma((3,)), dma, dma, dma,
        ],
        compiler_params=pltpu.CompilerParams(collective_id=0, has_side_effects=True),
        name="step",
    )(index, tiles, odd, x, cot, bias, first_weight, second_weight)


def finish_kernel(out_ref, all_ref, result_ref, first_ref, second_ref):
    result_ref[...] = out_ref[...]
    for kernel, target in ((0, first_ref), (1, second_ref)):
        for q in range(4):
            v = all_ref[kernel, q].astype(f32).reshape(128, 128)
            base, n = QROWS * q, min(QROWS, BLOCK - QROWS * q)
            target[base : base + n, 0:128] = v[0:n]
            target[base : base + n, 128:256] = v[48 : 48 + n]
            target[base : base + 24, 256:320] = v[96:120, 0:64]
            target[base + 24 : base + n, 256:320] = v[96 : 72 + n, 64:128]


def finish(out, everything):
    grad = jax.ShapeDtypeStruct((BLOCK, C), f32)
    return pl.pallas_call(
        finish_kernel,
        out_shape=(jax.ShapeDtypeStruct((PIX, C), bf16), grad, grad),
        in_specs=[VM, VM],
        out_specs=(VM, VM, VM),
        name="finish",
    )(out, everything)


def time_bias(timestep, time_weight):
    half_dim = TEMB // 2
    frequency = jnp.exp(-math.log(10000.0) * jnp.arange(half_dim, dtype=f32) / half_dim)
    angles = timestep.astype(f32) * frequency
    embedded = jnp.concatenate([jnp.cos(angles), jnp.sin(angles)])
    activated = jax.nn.silu(embedded).astype(bf16)
    return jnp.dot(activated[None, :], time_weight, preferred_element_type=f32)


def body(block_input, cotangent, timesteps, owner_map, time_weight, first_weight, second_weight):
    ids = jnp.arange(16, dtype=jnp.int32)
    inverse = jnp.sum((owner_map[None, :] == ids[:, None]).astype(jnp.int32) * ids[None, :], axis=1)
    quarter = lax.rem(lax.axis_index("rep") // 2, 4)
    starts = inverse * BLOCK + quarter.astype(jnp.int32) * QROWS
    bias = time_bias(timesteps[0], time_weight)
    x = block_input.reshape(PIX, C)
    cot = cotangent.reshape(PIX, C)
    out, everything = run_step(owner_map, starts // 8, lax.rem(starts // 4, 2), x, cot, bias, first_weight, second_weight)
    out, first_grad, second_grad = finish(out, everything)
    return out.reshape(1, HEIGHT, WIDTH, C), first_grad, second_grad


def solution(mesh):
    placed = (
        P(("rep", "dom"), None, None, None),
        P(("rep", "dom"), None, None, None),
        P(("rep", "dom")),
        P(),
        P(),
        P("dom", None),
        P("dom", None),
    )
    return jax.shard_map(
        body,
        mesh=mesh,
        in_specs=placed,
        out_specs=(P(("rep", "dom"), None, None, None), P("dom", None), P("dom", None)),
        check_vma=False,
    )
```

time: 1680 us -> 125 us (0.07)
  waiting for transfers between devices: 1490 us -> 0 us
  Pallas kernels: 0 us -> 121 us
  local copies, waits for them, and re-layouts: 102 us -> 0.67 us
  other arithmetic: 35.3 us -> 0.71 us
    psum x1 -> x0, waiting for transfers between devices: 800 us -> none  [body(): second_total, first_total = lax.psum((second_owned, total), 'rep')]
    all_gather x4 -> x0, waiting for transfers between devices: 691 us -> none  [the longest x1 252 us: body(): lax.all_gather(conv_grad.reshape(1, HEIGHT, WIDTH, C), 'dom', axis=0, til...]
    pallas_call x0 -> x2, Pallas kernels: none -> 121 us  [the longest x1 120 us: run_step(): pl.pallas_call(step_kernel, out_shape=(jax.ShapeDtypeStruct((PIX, C), bf1...]
    reshape x5 -> x0, local copies, waits for them, and re-layouts: 22.7 us -> none  [the longest x2 14.1 us: second_owner_sum(): term_rounded.reshape(group_size, block_rows, C)]
    dynamic_slice x33 -> x0, local copies, waits for them, and re-layouts: 17.1 us -> none  [the longest x16 14.5 us: body(): lax.scan(add_one, jnp.zeros((block_rows, C), jnp.float32), (act_piece, gr...]
  transfers between devices with their start and end apart: 6 -> 0, of which waited for: 5 -> 0; matrix products, arithmetic and copies ran while one was open for 9% -> 0% of each run, Pallas kernels for 0% -> 0%
where the time goes in v2:
time: 125 us
  Pallas kernels  121 us (97%)
  between operations  1.42 us (1%)
    pallas_call x1, Pallas kernels, run_step(): pl.pallas_call(step_kernel, out_shape=(jax.ShapeDtypeStruct((PIX, C), bf1...  120 us

profile of v2, /device:TPU:1, one launch (start us, length us, event | category | flops | bytes accessed | tf_op | source)
XLA Modules:
  0.0 125.1 jit_solution(13543584006961397626)
XLA Ops:
  0.6 0.0 copy-start
  1.4 0.0 copy-start.1
  1.4 0.6 copy-done.1
  2.0 0.1 select_reduce_fusion
  2.2 0.5 compare_select_fusion
  2.8 0.0 copy-done
  2.8 0.9 fusion.3.bias_ref
  3.7 119.6 %step.1 = (bf16[128,320]{1,0:T(8,128)(2,1)}, bf16[2,4,8,16,128]{4,3,2,1,0:T(8,128)(2,1)}) custom-call(s32[16]{0:T(128)} %index_ref.1, s32[16]{0:T(128)} %get-tuple-element.14.tile_ref, s32[16]{0:T(128)} %get-tuple-element.13.odd_ref, bf16[128,320]{1,0:T(8,128)(2,1)} %bitcast.6, bf16[128,320]{1,0:T(8,128)(2,1)} %bitcast.7, f32[1,320]{1,0:T(1,128)} %fusion.3.bias_ref, ...), custom_call_target="tpu_custom_call" | custom-call | tf_op jit(solution)/shard_map/step/pallas_call | solution.py:396
  123.2 1.9 %finish.1 = (bf16[128,320]{1,0:T(8,128)(2,1)}, f32[180,320]{1,0:T(8,128)}, f32[180,320]{1,0:T(8,128)}) custom-call(bf16[128,320]{1,0:T(8,128)(2,1)} %get-tuple-element.8.out_ref, bf16[2,4,8,16,128]{4,3,2,1,0:T(8,128)(2,1)} %get-tuple-element.9.all_ref), custom_call_target="tpu_custom_call" | custom-call | tf_op jit(solution)/shard_map/finish/pallas_call | solution.py:437
  (3 shorter events, 0.1 us)
Async XLA Ops:
  0.6 2.2 %copy-start = (bf16[1280,320]{0,1:T(8,128)(2,1)S(1)}, bf16[1280,320]{0,1:T(8,128)(2,1)}, u32[]{:S(2)}) copy-start(bf16[1280,320]{0,1:T(8,128)(2,1)} %param.11) | copy-start | bytes 2457604
  1.4 0.7 copy-start.1

commit v3 on v2

--- a/solution.py
+++ b/solution.py
@@ -65,10 +65,10 @@
         [w[0:96, 256:320], jnp.concatenate([w[96:180, 256:320], jnp.zeros((12, 64), f32)], axis=0)], axis=1
     )
     tiles = jnp.concatenate([w[:, 0:128], pad, w[:, 128:256], pad, fold, jnp.zeros((32, 128), f32)], axis=0)
-    return tiles.astype(bf16).reshape(4, 128, 128)
-
-
-def gather_weights(c, own, wg, keep, other, to_z, to_x, to_y, place, extra, zs, zr, so, ro, s2, r2, s3, r3, sc, rc):
+    return tiles.astype(bf16).reshape(4, 2, 64, 128)
+
+
+def gather_weights(c, own, wg, keep, other, to_z, to_x, to_y, place, extra, zs, zr, fs, fr, so, ro, s2, r2, s3, r3, sc, rc):
     x, z_hi, y = place
     sent = []
 
@@ -84,15 +84,20 @@
         return lax.rem(z_hi + 4 - d, 4)
 
     zc = {
-        d: go(own.at[c, x], wg.at[c, z_hi * 4 + y, x], zs.at[d - 1], zr.at[d - 1], to_z[d - 1])
-        for d in (2, 1, 3)
+        (d, h): go(own.at[c, x, h], wg.at[c, z_hi * 4 + y, x, h], zs.at[d - 1, h], zr.at[d - 1, h], to_z[d - 1])
+        for d, h in ((1, 1), (3, 0), (1, 0), (3, 1))
     }
     oc = [go(own.at[c], wg.at[c, z_hi * 4 + y], so.at[j], ro.at[j], to_y[j]) for j in (1, 0, 2)]
     extra(go)
     near, far = (to_x, to_y) if c == 0 else (to_y, to_x)
 
-    def second(d):
-        arrived([zc[d]])
+    def relay(d, h):
+        arrived([zc[d, h]])
+        part = wg.at[c, block(d) * 4 + y, x, h]
+        return go(part, part, fs.at[h], fr.at[h], to_z[d - 1])
+
+    def second(d, before):
+        arrived(before)
         part = wg.at[c, block(d) * 4 + y, x]
         return [go(part, part, s2.at[d - 1, j], r2.at[d - 1, j], near[j]) for j in (1, 0, 2)]
 
@@ -114,8 +119,10 @@
 
     for copy in keep:
         copy.wait()
-    a1 = second(1)
-    a3 = second(3)
+    upper = relay(1, 1)
+    lower = relay(3, 0)
+    a1 = second(1, [zc[1, 0]])
+    a3 = second(3, [zc[3, 1]])
     b1 = third(1, a1)
     b3 = third(3, a3)
     arrived(oc)
@@ -123,7 +130,7 @@
     for i in (1, 2, 3):
         part = wg.at[c, z_hi * 4 + lax.rem(y + i, 4)]
         last.append(go(part, part, sc.at[3 + i], rc.at[3 + i], other))
-    a2 = second(2)
+    a2 = second(2, [upper, lower])
     last += fourth(1, b1)
     b2 = third(2, a2)
     last += fourth(3, b3)
@@ -138,7 +145,7 @@
     out_ref, all_ref,
     own, wg, wl1, wl2, pad, act1, act2, cgrad, acts, grads, act_t, pads, total,
     part_ref, ybuf, s1, zbuf, s2b, hbuf, final,
-    own_sem, zs, zr, so, ro, s2, r2, s3, r3, sc, rc, sa, ra,
+    own_sem, zs, zr, fs, fr, so, ro, s2, r2, s3, r3, sc, rc, sa, ra,
     ys, yr, ls, lr, hs, hr, gs, gr, xs, xr, cs, cr, keep_sem,
 ):
     z_lo, x, core, z_hi, y = position()
@@ -214,7 +221,7 @@
 
             gather_weights(
                 c, own, wg, keep, other, to_z, to_x, to_y, (x, z_hi, y), extra,
-                zs, zr, so, ro, s2, r2, s3, r3, sc, rc,
+                zs, zr, fs, fr, so, ro, s2, r2, s3, r3, sc, rc,
             )
 
         pl.when(core == c)(run)
@@ -328,49 +335,47 @@
         product = jnp.dot(act_t[...], rows, preferred_element_type=f32)
         total[pl.ds((C // 8) * t, C // 8)] = product.reshape(C // 8, 8, C)
 
-    ycopies = []
-    for d in (2, 1, 3, 0):
-        column = lax.rem(y + d, 4)
-        for e in range(4):
-            first = tile_ref[e * 4 + column]
-            v = jnp.concatenate([total[first + i] for i in range(7)], axis=0)
-            late = jnp.full((48, C), odd_ref[e * 4 + column], jnp.int32) > 0
+    steps = (2, 1, 3, 0)
+    ycopies, lcopies, hcopies = [], [], []
+    for i, step in enumerate(steps):
+        holder = lax.rem(z_hi + step, 4)
+        ycopies.append([])
+        for d in (2, 1, 3, 0):
+            column = lax.rem(y + d, 4)
+            first = tile_ref[holder * 4 + column]
+            v = jnp.concatenate([total[first + n] for n in range(7)], axis=0)
+            late = jnp.full((48, C), odd_ref[holder * 4 + column], jnp.int32) > 0
             v = jnp.where(late, v[4:52], v[0:48])
             fold = jnp.concatenate([v[0:24, 256:320], v[24:48, 256:320]], axis=1)
             tile = jnp.concatenate([v[0:48, 0:128], v[0:48, 128:256], fold, jnp.zeros((8, 128), f32)], axis=0)
-            part_ref[column, e] = tile.astype(bf16).reshape(NZL, 16, 128)
-        if d > 0:
-            ycopies.append(
-                send(part_ref.at[column], ybuf.at[d - 1], ys.at[d - 1], yr.at[d - 1], to_y[d - 1])
-            )
-    for c in ycopies:
-        c.wait()
-    for e in range(NZH):
-        v = part_ref[y, e].astype(f32)
+            part_ref[i, column] = tile.astype(bf16).reshape(NZL, 16, 128)
+            if d > 0:
+                ycopies[i].append(
+                    send(part_ref.at[i, column], ybuf.at[d - 1, i], ys.at[d - 1, i], yr.at[d - 1, i], to_y[d - 1])
+                )
+    for i in range(4):
+        for c in ycopies[i]:
+            c.wait()
+        v = part_ref[i, y].astype(f32)
         for d in range(3):
-            v = v + ybuf[d, e].astype(f32)
-        s1[:, e] = v.astype(bf16)
-
-    copies = [
-        send(s1.at[lax.rem(z_lo + d, 8)], zbuf.at[d - 1], ls.at[d - 1], lr.at[d - 1], to_l[d - 1])
-        for d in (4, 3, 5, 2, 6, 1, 7)
-    ]
-    for c in copies:
-        c.wait()
-    v = s1[z_lo].astype(f32)
-    for d in range(7):
-        v = v + zbuf[d].astype(f32)
-    s2b[...] = v.astype(bf16)
-
-    copies = [
-        send(s2b.at[lax.rem(z_hi + d, 4)], hbuf.at[d - 1], hs.at[d - 1], hr.at[d - 1], to_z[d - 1])
-        for d in (2, 1, 3)
-    ]
-    for c in copies:
-        c.wait()
-    v = s2b[z_hi].astype(f32)
-    for d in range(3):
-        v = v + hbuf[d].astype(f32)
+            v = v + ybuf[d, i].astype(f32)
+        s1[i] = v.astype(bf16)
+        lcopies.append([
+            send(s1.at[i, lax.rem(z_lo + d, 8)], zbuf.at[d - 1, i], ls.at[d - 1, i], lr.at[d - 1, i], to_l[d - 1])
+            for d in (4, 3, 5, 2, 6, 1, 7)
+        ])
+    for i, step in enumerate(steps):
+        for c in lcopies[i]:
+            c.wait()
+        v = s1[i, z_lo].astype(f32)
+        for d in range(7):
+            v = v + zbuf[d, i].astype(f32)
+        if step > 0:
+            s2b[i] = v.astype(bf16)
+            hcopies.append(send(s2b.at[i], hbuf.at[i], hs.at[i], hr.at[i], to_z[step - 1]))
+    for i in (1, 2, 0):
+        hcopies[i].wait()
+        v = v + hbuf[i].astype(f32)
     final[...] = (v * (1.0 / SAMPLES)).astype(bf16)
 
     kept = pltpu.make_async_copy(final, all_ref.at[core, x, z_lo], keep_sem)
@@ -402,17 +407,17 @@
         in_specs=[SM, SM, SM, VM, VM, VM, VM, VM],
         out_specs=(VM, VM),
         scratch_shapes=[
-            v((2, 4, 128, 128), bf16), v((2, NZH * NY, 4, 128, 128), bf16),
+            v((2, 4, 2, 64, 128), bf16), v((2, NZH * NY, 4, 2, 64, 128), bf16),
             v((9 * C, C), bf16), v((9 * C, C), bf16), v((3, 160, C), bf16),
             v((PIX, C), bf16), v((PIX, C), bf16), v((PIX, C), bf16),
             v((8, PIX, C), bf16), v((8, PIX, C), bf16), v((C, 8 * PIX), bf16),
             v((3, 8, 160, C), bf16), v((9 * C // 8 + 3, 8, C), f32),
-            v((NY, NZH, NZL, 16, 128), bf16), v((3, NZH, NZL, 16, 128), bf16),
-            v((NZL, NZH, 16, 128), bf16), v((7, NZH, 16, 128), bf16), v((NZH, 16, 128), bf16),
+            v((NZH, NY, NZL, 16, 128), bf16), v((3, NZH, NZL, 16, 128), bf16),
+            v((NZH, NZL, 16, 128), bf16), v((7, NZH, 16, 128), bf16), v((3, 16, 128), bf16),
             v((3, 16, 128), bf16), v((16, 128), bf16),
-            dma((2,)), dma((3,)), dma((3,)), dma((3,)), dma((3,)), dma((3, 3)), dma((3, 3)),
+            dma((2,)), dma((3, 2)), dma((3, 2)), dma((2,)), dma((2,)), dma((3,)), dma((3,)), dma((3, 3)), dma((3, 3)),
             dma((3, 4, 3)), dma((3, 4, 3)), dma((7,)), dma((7,)), dma((4, 4)), dma((2, 4, 2)),
-            dma((3,)), dma((3,)), dma((7,)), dma((7,)), dma((3,)), dma((3,)),
+            dma((3, 4)), dma((3, 4)), dma((7, 4)), dma((7, 4)), dma((3,)), dma((3,)),
             dma((7,)), dma((7,)), dma((3,)), dma((3,)), dma, dma, dma,
         ],
         compiler_params=pltpu.CompilerParams(collective_id=0, has_side_effects=True),

time: 125 us -> 122 us (0.976)
  Pallas kernels: 121 us -> 118 us
    pallas_call x1, Pallas kernels: 120 us -> 116 us  [run_step(): pl.pallas_call(step_kernel, out_shape=(jax.ShapeDtypeStruct((PIX, C), bf1...]
where the time goes in v3:
time: 122 us
  Pallas kernels  118 us (97%)
  between operations  1.42 us (1%)
    pallas_call x1, Pallas kernels, run_step(): pl.pallas_call(step_kernel, out_shape=(jax.ShapeDtypeStruct((PIX, C), bf1...  116 us

profile of v3, /device:TPU:1, one launch (start us, length us, event | category | flops | bytes accessed | tf_op | source)
XLA Modules:
  0.0 122.0 jit_solution(14185095125871899879)
XLA Ops:
  0.6 0.0 copy-start
  1.4 0.0 copy-start.1
  1.4 0.6 copy-done.1
  2.0 0.1 select_reduce_fusion
  2.2 0.5 compare_select_fusion
  2.8 0.0 copy-done
  2.8 0.9 fusion.3.bias_ref
  3.7 116.4 %step.1 = (bf16[128,320]{1,0:T(8,128)(2,1)}, bf16[2,4,8,16,128]{4,3,2,1,0:T(8,128)(2,1)}) custom-call(s32[16]{0:T(128)} %index_ref.1, s32[16]{0:T(128)} %get-tuple-element.14.tile_ref, s32[16]{0:T(128)} %get-tuple-element.13.odd_ref, bf16[128,320]{1,0:T(8,128)(2,1)} %bitcast.6, bf16[128,320]{1,0:T(8,128)(2,1)} %bitcast.7, f32[1,320]{1,0:T(1,128)} %fusion.3.bias_ref, ...), custom_call_target="tpu_custom_call" | custom-call | tf_op jit(solution)/shard_map/step/pallas_call | solution.py:401
  120.1 1.9 %finish.1 = (bf16[128,320]{1,0:T(8,128)(2,1)}, f32[180,320]{1,0:T(8,128)}, f32[180,320]{1,0:T(8,128)}) custom-call(bf16[128,320]{1,0:T(8,128)(2,1)} %get-tuple-element.8.out_ref, bf16[2,4,8,16,128]{4,3,2,1,0:T(8,128)(2,1)} %get-tuple-element.9.all_ref), custom_call_target="tpu_custom_call" | custom-call | tf_op jit(solution)/shard_map/finish/pallas_call | solution.py:442
  (3 shorter events, 0.1 us)
Async XLA Ops:
  0.6 2.2 %copy-start = (bf16[1280,320]{0,1:T(8,128)(2,1)S(1)}, bf16[1280,320]{0,1:T(8,128)(2,1)}, u32[]{:S(2)}) copy-start(bf16[1280,320]{0,1:T(8,128)(2,1)} %param.11) | copy-start | bytes 2457604
  1.4 0.7 copy-start.1

commit v4 on v3

--- a/solution.py
+++ b/solution.py
@@ -84,7 +84,7 @@
         return lax.rem(z_hi + 4 - d, 4)
 
     zc = {
-        (d, h): go(own.at[c, x, h], wg.at[c, z_hi * 4 + y, x, h], zs.at[d - 1, h], zr.at[d - 1, h], to_z[d - 1])
+        (d, h): go(own.at[c, x, h], wg.at[c, z_hi * 4 + y, x, h], zs.at[d - 1, h], zr.at[d - 1, h], to_z[d])
         for d, h in ((1, 1), (3, 0), (1, 0), (3, 1))
     }
     oc = [go(own.at[c], wg.at[c, z_hi * 4 + y], so.at[j], ro.at[j], to_y[j]) for j in (1, 0, 2)]
@@ -94,7 +94,7 @@
     def relay(d, h):
         arrived([zc[d, h]])
         part = wg.at[c, block(d) * 4 + y, x, h]
-        return go(part, part, fs.at[h], fr.at[h], to_z[d - 1])
+        return go(part, part, fs.at[h], fr.at[h], to_z[d])
 
     def second(d, before):
         arrived(before)
@@ -150,13 +150,13 @@
 ):
     z_lo, x, core, z_hi, y = position()
     slot = x * 2 + core
-    to_z = [device(z_lo, x, core, lax.rem(z_hi + d, 4), y) for d in (1, 2, 3)]
+    to_z = {d: device(z_lo, x, core, lax.rem(z_hi + d, 4), y) for d in (1, 3)}
     to_y = [device(z_lo, x, core, z_hi, lax.rem(y + d, 4)) for d in (1, 2, 3)]
     to_l = [device(lax.rem(z_lo + d, 8), x, core, z_hi, y) for d in range(1, 8)]
     at_x = [[device(z_lo, lax.rem(x + d, 4), c, z_hi, y) for d in (1, 2, 3)] for c in (0, 1)]
     to_x = [device(z_lo, lax.rem(x + d, 4), core, z_hi, y) for d in (1, 2, 3)]
     other = device(z_lo, x, 1 - core, z_hi, y)
-    partners = to_z + to_y + to_l + at_x[0] + at_x[1] + [other]
+    partners = [to_z[1], to_z[3]] + to_y + to_l + at_x[0] + at_x[1] + [other]
     barrier = pltpu.get_barrier_semaphore()
     for partner in partners:
         pl.semaphore_signal(barrier, inc=1, device_id=partner, device_id_type=MESH)
@@ -271,10 +271,17 @@
             (((1,), (1,)), ((), ())), preferred_element_type=f32,
         )
     norm_grad = act_grad * gate * (1.0 + second_norm * (1.0 - gate))
-    cgrad[...] = (
-        second_std
-        * (norm_grad - group_mean(norm_grad) - second_norm * group_mean(norm_grad * second_norm))
-    ).astype(bf16)
+    columns = jnp.concatenate(
+        [
+            jnp.broadcast_to(jnp.sum(norm_grad, axis=0, keepdims=True), (8, C)),
+            jnp.broadcast_to(jnp.sum(norm_grad * second_norm, axis=0, keepdims=True), (8, C)),
+        ],
+        axis=0,
+    )
+    means = count * jnp.dot(
+        columns, member, precision=lax.Precision.HIGHEST, preferred_element_type=f32
+    )
+    cgrad[...] = (second_std * (norm_grad - means[0:1] - second_norm * means[8:9])).astype(bf16)
 
     @pl.when(core == 0)
     def _():
@@ -336,7 +343,7 @@
         total[pl.ds((C // 8) * t, C // 8)] = product.reshape(C // 8, 8, C)
 
     steps = (2, 1, 3, 0)
-    ycopies, lcopies, hcopies = [], [], []
+    ycopies, lcopies, hcopies = [], [], {}
     for i, step in enumerate(steps):
         holder = lax.rem(z_hi + step, 4)
         ycopies.append([])
@@ -364,16 +371,22 @@
             send(s1.at[i, lax.rem(z_lo + d, 8)], zbuf.at[d - 1, i], ls.at[d - 1, i], lr.at[d - 1, i], to_l[d - 1])
             for d in (4, 3, 5, 2, 6, 1, 7)
         ])
-    for i, step in enumerate(steps):
+    for i, step in ((0, 2), (2, 3), (3, 0), (1, 1)):
         for c in lcopies[i]:
             c.wait()
         v = s1[i, z_lo].astype(f32)
         for d in range(7):
             v = v + zbuf[d, i].astype(f32)
-        if step > 0:
+        if step == 0:
+            own_sum = v
+        else:
+            if step == 1:
+                hcopies[0].wait()
+                v = v + hbuf[0].astype(f32)
             s2b[i] = v.astype(bf16)
-            hcopies.append(send(s2b.at[i], hbuf.at[i], hs.at[i], hr.at[i], to_z[step - 1]))
-    for i in (1, 2, 0):
+            hcopies[i] = send(s2b.at[i], hbuf.at[i], hs.at[i], hr.at[i], to_z[3 if step == 3 else 1])
+    v = own_sum
+    for i in (2, 1):
         hcopies[i].wait()
         v = v + hbuf[i].astype(f32)
     final[...] = (v * (1.0 / SAMPLES)).astype(bf16)

time: 122 us -> 120 us (0.984)
  Pallas kernels: 118 us -> 116 us
    pallas_call x1, Pallas kernels: 116 us -> 114 us  [run_step(): pl.pallas_call(step_kernel, out_shape=(jax.ShapeDtypeStruct((PIX, C), bf1...]
where the time goes in v4:
time: 120 us
  Pallas kernels  116 us (97%)
  between operations  1.42 us (1%)
    pallas_call x1, Pallas kernels, run_step(): pl.pallas_call(step_kernel, out_shape=(jax.ShapeDtypeStruct((PIX, C), bf1...  114 us

profile of v4, /device:TPU:1, one launch (start us, length us, event | category | flops | bytes accessed | tf_op | source)
XLA Modules:
  0.0 119.7 jit_solution(9166980906005121717)
XLA Ops:
  0.6 0.0 copy-start
  1.4 0.0 copy-start.1
  1.4 0.6 copy-done.1
  2.0 0.1 select_reduce_fusion
  2.2 0.5 compare_select_fusion
  2.8 0.0 copy-done
  2.8 0.9 fusion.3.bias_ref
  3.7 114.1 %step.1 = (bf16[128,320]{1,0:T(8,128)(2,1)}, bf16[2,4,8,16,128]{4,3,2,1,0:T(8,128)(2,1)}) custom-call(s32[16]{0:T(128)} %index_ref.1, s32[16]{0:T(128)} %get-tuple-element.14.tile_ref, s32[16]{0:T(128)} %get-tuple-element.13.odd_ref, bf16[128,320]{1,0:T(8,128)(2,1)} %bitcast.6, bf16[128,320]{1,0:T(8,128)(2,1)} %bitcast.7, f32[1,320]{1,0:T(1,128)} %fusion.3.bias_ref, ...), custom_call_target="tpu_custom_call" | custom-call | tf_op jit(solution)/shard_map/step/pallas_call | solution.py:414
  117.8 1.9 %finish.1 = (bf16[128,320]{1,0:T(8,128)(2,1)}, f32[180,320]{1,0:T(8,128)}, f32[180,320]{1,0:T(8,128)}) custom-call(bf16[128,320]{1,0:T(8,128)(2,1)} %get-tuple-element.8.out_ref, bf16[2,4,8,16,128]{4,3,2,1,0:T(8,128)(2,1)} %get-tuple-element.9.all_ref), custom_call_target="tpu_custom_call" | custom-call | tf_op jit(solution)/shard_map/finish/pallas_call | solution.py:455
  (3 shorter events, 0.1 us)
Async XLA Ops:
  0.6 2.2 %copy-start = (bf16[1280,320]{0,1:T(8,128)(2,1)S(1)}, bf16[1280,320]{0,1:T(8,128)(2,1)}, u32[]{:S(2)}) copy-start(bf16[1280,320]{0,1:T(8,128)(2,1)} %param.11) | copy-start | bytes 2457604
  1.4 0.7 copy-start.1

commit v5 on v4

--- a/solution.py
+++ b/solution.py
@@ -58,6 +58,17 @@
     return jnp.where(inside, pltpu.roll(v, (-step) % rows, 0), 0.0)
 
 
+def pack_map(v):
+    fold = jnp.concatenate([v[0:64, 256:320], v[64:128, 256:320]], axis=1)
+    return jnp.concatenate([v[:, 0:128], v[:, 128:256], fold], axis=0).astype(bf16)
+
+
+def unpack_map(p):
+    p = p.astype(f32)
+    tail = jnp.concatenate([p[256:320, 0:64], p[256:320, 64:128]], axis=0)
+    return jnp.concatenate([p[0:128], p[128:256], tail], axis=1)
+
+
 def pack_block(w):
     w = w.astype(f32)
     pad = jnp.zeros((12, 128), f32)
@@ -105,17 +116,24 @@
         arrived(before)
         if c == 0:
             part = wg.at[0, block(d) * 4 + y]
-            return [go(part, part, s3.at[d - 1, 0, j], r3.at[d - 1, 0, j], far[j]) for j in (1, 0, 2)]
+            return {j + 1: go(part, part, s3.at[d - 1, 0, j], r3.at[d - 1, 0, j], far[j]) for j in (1, 0, 2)}
+        copies = {}
+        for i in range(4):
+            part = wg.at[1, block(d) * 4 + lax.rem(y + i, 4), x]
+            for j in (1, 0, 2):
+                copies[i, j] = go(part, part, s3.at[d - 1, i, j], r3.at[d - 1, i, j], far[j])
+        return copies
+
+    def fourth(d, before):
         copies = []
         for i in range(4):
-            part = wg.at[1, block(d) * 4 + lax.rem(y + i, 4), x]
-            copies += [go(part, part, s3.at[d - 1, i, j], r3.at[d - 1, i, j], far[j]) for j in (1, 0, 2)]
+            if c == 0:
+                arrived([before[4 - i]] if i > 0 else [])
+            else:
+                arrived([before[i, j] for j in range(3)])
+            part = wg.at[c, block(d) * 4 + lax.rem(y + i, 4)]
+            copies.append(go(part, part, sc.at[d, i], rc.at[d, i], other))
         return copies
-
-    def fourth(d, before):
-        arrived(before)
-        part = wg.at[c, pl.ds(block(d) * 4, 4)]
-        return [go(part, part, sc.at[d], rc.at[d], other)]
 
     for copy in keep:
         copy.wait()
@@ -129,7 +147,7 @@
     last = []
     for i in (1, 2, 3):
         part = wg.at[c, z_hi * 4 + lax.rem(y + i, 4)]
-        last.append(go(part, part, sc.at[3 + i], rc.at[3 + i], other))
+        last.append(go(part, part, sc.at[0, i], rc.at[0, i], other))
     a2 = second(2, [upper, lower])
     last += fourth(1, b1)
     b2 = third(2, a2)
@@ -143,7 +161,7 @@
 def step_kernel(
     index_ref, tile_ref, odd_ref, x_ref, cot_ref, bias_ref, w1_ref, w2_ref,
     out_ref, all_ref,
-    own, wg, wl1, wl2, pad, act1, act2, cgrad, acts, grads, act_t, pads, total,
+    own, wg, wl1, wl2, pad, act1, act2, cgrad, cots, acts, grads, act_t, pads, total,
     part_ref, ybuf, s1, zbuf, s2b, hbuf, final,
     own_sem, zs, zr, fs, fr, so, ro, s2, r2, s3, r3, sc, rc, sa, ra,
     ys, yr, ls, lr, hs, hr, gs, gr, xs, xr, cs, cr, keep_sem,
@@ -180,7 +198,9 @@
     own[1] = pack_block(w2_ref[...])
     source = x_ref[...].astype(f32)
     normed, _ = group_norm(source)
-    act1[...] = (normed * (1.0 / (1.0 + jnp.exp(-normed)))).astype(bf16)
+    first_act = (normed * (1.0 / (1.0 + jnp.exp(-normed)))).astype(bf16).astype(f32)
+    act1[...] = pack_map(first_act)
+    cots[...] = pack_map(cot_ref[...].astype(f32))
     pad[:, 0:16, :] = jnp.zeros((3, 16, C), bf16)
     pad[:, 144:160, :] = jnp.zeros((3, 16, C), bf16)
     pads[:, :, 0:16, :] = jnp.zeros((3, 8, 16, C), bf16)
@@ -191,7 +211,7 @@
         for k in range(3):
             pad[k, 16:144, :] = shifted(v, k - 1, PIX).astype(bf16)
 
-    fill(act1[...].astype(f32))
+    fill(first_act)
 
     @pl.when(core == 0)
     def _():
@@ -199,7 +219,7 @@
 
     @pl.when(core == 1)
     def _():
-        grads[slot] = cot_ref[...]
+        grads[slot] = cots[...]
 
     pl.semaphore_wait(barrier, len(partners))
 
@@ -213,11 +233,11 @@
             def extra(go):
                 for j in (1, 0, 2):
                     go(act1, acts.at[slot], sa.at[0, j + 1], ra.at[0, j + 1, c], at_x[0][j])
-                    go(cot_ref, grads.at[slot], sa.at[2, j + 1], ra.at[1, j + 1, c], at_x[1][j])
+                    go(cots, grads.at[slot], sa.at[2, j + 1], ra.at[1, j + 1, c], at_x[1][j])
                 if c == 1:
                     go(act1, acts.at[slot], sa.at[0, 0], ra.at[0, 0, 1], other)
                 else:
-                    go(cot_ref, grads.at[slot], sa.at[2, 0], ra.at[1, 0, 0], other)
+                    go(cots, grads.at[slot], sa.at[2, 0], ra.at[1, 0, 0], other)
 
             gather_weights(
                 c, own, wg, keep, other, to_z, to_x, to_y, (x, z_hi, y), extra,
@@ -247,8 +267,8 @@
 
     second_norm, second_std = group_norm(conv(wl1) + bias_ref[...])
     gate = 1.0 / (1.0 + jnp.exp(-second_norm))
-    second_act = (second_norm * gate).astype(bf16)
-    act2[...] = second_act
+    second_act = (second_norm * gate).astype(bf16).astype(f32)
+    act2[...] = pack_map(second_act)
 
     @pl.when(core == 1)
     def _():
@@ -281,7 +301,7 @@
     means = count * jnp.dot(
         columns, member, precision=lax.Precision.HIGHEST, preferred_element_type=f32
     )
-    cgrad[...] = (second_std * (norm_grad - means[0:1] - second_norm * means[8:9])).astype(bf16)
+    cgrad[...] = pack_map(second_std * (norm_grad - means[0:1] - second_norm * means[8:9]))
 
     @pl.when(core == 0)
     def _():
@@ -295,7 +315,7 @@
     def _():
         send(cgrad, grads.at[slot], sa.at[3, 0], ra.at[1, 0, 1], other)
 
-    fill(act2[...].astype(f32))
+    fill(unpack_map(act2[...]))
     out_ref[...] = (x_ref[...].astype(f32) + conv(wl2)).astype(bf16)
 
     def take_acts():
@@ -306,7 +326,7 @@
 
         @pl.loop(0, 8)
         def _(s):
-            act_t[:, pl.ds(pl.multiple_of(PIX * s, PIX), PIX)] = acts[s].astype(f32).T.astype(bf16)
+            act_t[:, pl.ds(pl.multiple_of(PIX * s, PIX), PIX)] = unpack_map(acts[s]).T.astype(bf16)
 
     def take_grads():
         for d in (1, 2, 3):
@@ -316,7 +336,7 @@
 
         @pl.loop(0, 8)
         def _(s):
-            v = grads[s].astype(f32)
+            v = unpack_map(grads[s])
             for k in range(3):
                 pads[k, s, 16:144, :] = shifted(v, k - 1, PIX).astype(bf16)
 
@@ -422,14 +442,14 @@
         scratch_shapes=[
             v((2, 4, 2, 64, 128), bf16), v((2, NZH * NY, 4, 2, 64, 128), bf16),
             v((9 * C, C), bf16), v((9 * C, C), bf16), v((3, 160, C), bf16),
-            v((PIX, C), bf16), v((PIX, C), bf16), v((PIX, C), bf16),
-            v((8, PIX, C), bf16), v((8, PIX, C), bf16), v((C, 8 * PIX), bf16),
+            v((C, 128), bf16), v((C, 128), bf16), v((C, 128), bf16), v((C, 128), bf16),
+            v((8, C, 128), bf16), v((8, C, 128), bf16), v((C, 8 * PIX), bf16),
             v((3, 8, 160, C), bf16), v((9 * C // 8 + 3, 8, C), f32),
             v((NZH, NY, NZL, 16, 128), bf16), v((3, NZH, NZL, 16, 128), bf16),
             v((NZH, NZL, 16, 128), bf16), v((7, NZH, 16, 128), bf16), v((3, 16, 128), bf16),
             v((3, 16, 128), bf16), v((16, 128), bf16),
             dma((2,)), dma((3, 2)), dma((3, 2)), dma((2,)), dma((2,)), dma((3,)), dma((3,)), dma((3, 3)), dma((3, 3)),
-            dma((3, 4, 3)), dma((3, 4, 3)), dma((7,)), dma((7,)), dma((4, 4)), dma((2, 4, 2)),
+            dma((3, 4, 3)), dma((3, 4, 3)), dma((4, 4)), dma((4, 4)), dma((4, 4)), dma((2, 4, 2)),
             dma((3, 4)), dma((3, 4)), dma((7, 4)), dma((7, 4)), dma((3,)), dma((3,)),
             dma((7,)), dma((7,)), dma((3,)), dma((3,)), dma, dma, dma,
         ],

time: 120 us -> 119 us (level)
    pallas_call x1, Pallas kernels: 114 us -> 113 us  [run_step(): pl.pallas_call(step_kernel, out_shape=(jax.ShapeDtypeStruct((PIX, C), bf1...]
where the time goes in v5:
time: 119 us; the launch traced here: 118 us
  Pallas kernels  115 us (97%)
  between operations  1.42 us (1%)
    pallas_call x1, Pallas kernels, run_step(): pl.pallas_call(step_kernel, out_shape=(jax.ShapeDtypeStruct((PIX, C), bf1...  113 us

profile of v5, /device:TPU:1, one launch (start us, length us, event | category | flops | bytes accessed | tf_op | source)
XLA Modules:
  0.0 118.4 jit_solution(4827872602075362551)
XLA Ops:
  0.6 0.0 copy-start
  1.4 0.0 copy-start.1
  1.4 0.6 copy-done.1
  2.0 0.1 select_reduce_fusion
  2.2 0.5 compare_select_fusion
  2.8 0.0 copy-done
  2.8 0.9 fusion.3.bias_ref
  3.7 112.8 %step.1 = (bf16[128,320]{1,0:T(8,128)(2,1)}, bf16[2,4,8,16,128]{4,3,2,1,0:T(8,128)(2,1)}) custom-call(s32[16]{0:T(128)} %index_ref.1, s32[16]{0:T(128)} %get-tuple-element.14.tile_ref, s32[16]{0:T(128)} %get-tuple-element.13.odd_ref, bf16[128,320]{1,0:T(8,128)(2,1)} %bitcast.6, bf16[128,320]{1,0:T(8,128)(2,1)} %bitcast.7, f32[1,320]{1,0:T(1,128)} %fusion.3.bias_ref, ...), custom_call_target="tpu_custom_call" | custom-call | tf_op jit(solution)/shard_map/step/pallas_call | solution.py:434
  116.5 1.9 %finish.1 = (bf16[128,320]{1,0:T(8,128)(2,1)}, f32[180,320]{1,0:T(8,128)}, f32[180,320]{1,0:T(8,128)}) custom-call(bf16[128,320]{1,0:T(8,128)(2,1)} %get-tuple-element.8.out_ref, bf16[2,4,8,16,128]{4,3,2,1,0:T(8,128)(2,1)} %get-tuple-element.9.all_ref), custom_call_target="tpu_custom_call" | custom-call | tf_op jit(solution)/shard_map/finish/pallas_call | solution.py:475
  (3 shorter events, 0.1 us)
Async XLA Ops:
  0.6 2.2 %copy-start = (bf16[1280,320]{0,1:T(8,128)(2,1)S(1)}, bf16[1280,320]{0,1:T(8,128)(2,1)}, u32[]{:S(2)}) copy-start(bf16[1280,320]{0,1:T(8,128)(2,1)} %param.11) | copy-start | bytes 2457604
  1.4 0.7 copy-start.1

commit v6 on v5

--- a/solution.py
+++ b/solution.py
@@ -421,11 +421,16 @@
     for c in copies:
         c.wait()
     quarter = all_ref.at[core, x]
-    copies = [send(quarter, quarter, xs.at[d - 1], xr.at[d - 1], to_x[d - 1]) for d in (2, 1, 3)]
-    for c in copies:
+    copies = {d: send(quarter, quarter, xs.at[d - 1], xr.at[d - 1], to_x[d - 1]) for d in (2, 1, 3)}
+    forwards = [send(quarter, quarter, cs.at[0], cr.at[0], other)]
+    for d in (1, 3, 2):
+        copies[d].wait_recv()
+        part = all_ref.at[core, lax.rem(x + 4 - d, 4)]
+        forwards.append(send(part, part, cs.at[d], cr.at[d], other))
+    for d in (1, 3, 2):
+        copies[d].wait_send()
+    for c in forwards:
         c.wait()
-    whole = all_ref.at[core]
-    send(whole, whole, cs, cr, other).wait()
 
 
 def run_step(index, tiles, odd, x, cot, bias, first_weight, second_weight):
@@ -451,7 +456,7 @@
             dma((2,)), dma((3, 2)), dma((3, 2)), dma((2,)), dma((2,)), dma((3,)), dma((3,)), dma((3, 3)), dma((3, 3)),
             dma((3, 4, 3)), dma((3, 4, 3)), dma((4, 4)), dma((4, 4)), dma((4, 4)), dma((2, 4, 2)),
             dma((3, 4)), dma((3, 4)), dma((7, 4)), dma((7, 4)), dma((3,)), dma((3,)),
-            dma((7,)), dma((7,)), dma((3,)), dma((3,)), dma, dma, dma,
+            dma((7,)), dma((7,)), dma((3,)), dma((3,)), dma((4,)), dma((4,)), dma,
         ],
         compiler_params=pltpu.CompilerParams(collective_id=0, has_side_effects=True),
         name="step",

time: 119 us -> 118 us (level)
  no operation moved by 1% of the time
where the time goes in v6:
time: 118 us
  Pallas kernels  115 us (97%)
  between operations  1.42 us (1%)
    pallas_call x1, Pallas kernels, run_step(): pl.pallas_call(step_kernel, out_shape=(jax.ShapeDtypeStruct((PIX, C), bf1...  113 us

profile of v6, /device:TPU:1, one launch (start us, length us, event | category | flops | bytes accessed | tf_op | source)
XLA Modules:
  0.0 118.3 jit_solution(1372946504159240594)
XLA Ops:
  0.6 0.0 copy-start
  1.4 0.0 copy-start.1
  1.4 0.6 copy-done.1
  2.0 0.1 select_reduce_fusion
  2.2 0.5 compare_select_fusion
  2.8 0.0 copy-done
  2.8 0.9 fusion.3.bias_ref
  3.7 112.7 %step.1 = (bf16[128,320]{1,0:T(8,128)(2,1)}, bf16[2,4,8,16,128]{4,3,2,1,0:T(8,128)(2,1)}) custom-call(s32[16]{0:T(128)} %index_ref.1, s32[16]{0:T(128)} %get-tuple-element.14.tile_ref, s32[16]{0:T(128)} %get-tuple-element.13.odd_ref, bf16[128,320]{1,0:T(8,128)(2,1)} %bitcast.6, bf16[128,320]{1,0:T(8,128)(2,1)} %bitcast.7, f32[1,320]{1,0:T(1,128)} %fusion.3.bias_ref, ...), custom_call_target="tpu_custom_call" | custom-call | tf_op jit(solution)/shard_map/step/pallas_call | solution.py:439
  116.4 1.9 %finish.1 = (bf16[128,320]{1,0:T(8,128)(2,1)}, f32[180,320]{1,0:T(8,128)}, f32[180,320]{1,0:T(8,128)}) custom-call(bf16[128,320]{1,0:T(8,128)(2,1)} %get-tuple-element.8.out_ref, bf16[2,4,8,16,128]{4,3,2,1,0:T(8,128)(2,1)} %get-tuple-element.9.all_ref), custom_call_target="tpu_custom_call" | custom-call | tf_op jit(solution)/shard_map/finish/pallas_call | solution.py:480
  (3 shorter events, 0.1 us)
Async XLA Ops:
  0.6 2.2 %copy-start = (bf16[1280,320]{0,1:T(8,128)(2,1)S(1)}, bf16[1280,320]{0,1:T(8,128)(2,1)}, u32[]{:S(2)}) copy-start(bf16[1280,320]{0,1:T(8,128)(2,1)} %param.11) | copy-start | bytes 2457604
  1.4 0.7 copy-start.1
